TPU v7x, 32 devices: a whole 2x2x4 slice. The times are simulated.
32 devices in a mesh: dp: 8 (over z, y), tensor: 4 (over x, core).
Axes of the slice: x: 2, y: 2, z: 4, core: 2. Of those that a mesh axis runs over, the one named last changes fastest.
Arguments:
- hidden_in: bfloat16 [24576, 768], P(('dp', 'tensor')), may hold values from -6 to 6
- cotangent: bfloat16 [24576, 768], P(('dp', 'tensor')), may hold values from -6 to 6
- lengths: int32 [8, 2, 3], P('dp'), may hold values from 1 to 1024, 1536 in all within a row
- deal: int32 [24576], P('dp'), may hold values from 0 to 24575, as said below
- inverse: int32 [24576], P('dp'), may hold values from 0 to 24575, as said below
- micro: int32 [8, 2], P('dp'), may hold values from 0 to 1, as said below
- qkv_weight: float32 [2, 768, 3, 768], P(None, 'dp', None, 'tensor'), may hold values from -0.21875 to 0.21875
- proj_weight: float32 [2, 768, 768], P(None, 'dp', 'tensor'), may hold values from -2.5 to 2.5
- gate_up_weight: float32 [2, 768, 2, 3072], P(None, 'dp', None, 'tensor'), may hold values from -0.21875 to 0.21875
- down_weight: float32 [2, 768, 3072], P(None, 'dp', 'tensor'), may hold values from -0.109375 to 0.109375
- norm_params: float32 [2, 4, 768], replicated, may hold values from -0.9 to 1.45, as said below
- qkv_momentum: float32 [2, 768, 3, 768], P(None, 'dp', None, 'tensor'), may hold values from -256 to 256
- proj_momentum: float32 [2, 768, 768], P(None, 'dp', 'tensor'), may hold values from -256 to 256
- gate_up_momentum: float32 [2, 768, 2, 3072], P(None, 'dp', None, 'tensor'), may hold values from -256 to 256
- down_momentum: float32 [2, 768, 3072], P(None, 'dp', 'tensor'), may hold values from -256 to 256
- norm_momentum: float32 [2, 4, 768], replicated, may hold values from -896 to 896
- qkv_average: float32 [2, 768, 3, 768], P(None, 'dp', None, 'tensor'), may hold values from -0.21875 to 0.21875
- proj_average: float32 [2, 768, 768], P(None, 'dp', 'tensor'), may hold values from -2.5 to 2.5
- gate_up_average: float32 [2, 768, 2, 3072], P(None, 'dp', None, 'tensor'), may hold values from -0.21875 to 0.21875
- down_average: float32 [2, 768, 3072], P(None, 'dp', 'tensor'), may hold values from -0.109375 to 0.109375
- norm_average: float32 [2, 4, 768], replicated, may hold values from 0.5 to 1.5
Outputs:
- block_out: float32 [24576, 768], P(('dp', 'tensor'))
- input_grad: float32 [24576, 768], P(('dp', 'tensor'))
- qkv_grad: float32 [2, 768, 3, 768], P(None, 'dp', None, 'tensor')
- qkv_new: float32 [2, 768, 3, 768], P(None, 'dp', None, 'tensor')
- qkv_momentum_new: float32 [2, 768, 3, 768], P(None, 'dp', None, 'tensor')
- qkv_average_new: float32 [2, 768, 3, 768], P(None, 'dp', None, 'tensor')
- proj_grad: float32 [2, 768, 768], P(None, 'dp', 'tensor')
- proj_new: float32 [2, 768, 768], P(None, 'dp', 'tensor')
- proj_momentum_new: float32 [2, 768, 768], P(None, 'dp', 'tensor')
- proj_average_new: float32 [2, 768, 768], P(None, 'dp', 'tensor')
- gate_up_grad: float32 [2, 768, 2, 3072], P(None, 'dp', None, 'tensor')
- gate_up_new: float32 [2, 768, 2, 3072], P(None, 'dp', None, 'tensor')
- gate_up_momentum_new: float32 [2, 768, 2, 3072], P(None, 'dp', None, 'tensor')
- gate_up_average_new: float32 [2, 768, 2, 3072], P(None, 'dp', None, 'tensor')
- down_grad: float32 [2, 768, 3072], P(None, 'dp', 'tensor')
- down_new: float32 [2, 768, 3072], P(None, 'dp', 'tensor')
- down_momentum_new: float32 [2, 768, 3072], P(None, 'dp', 'tensor')
- down_average_new: float32 [2, 768, 3072], P(None, 'dp', 'tensor')
- norm_grad: float32 [2, 4, 768], replicated
- norm_new: float32 [2, 4, 768], replicated
- norm_momentum_new: float32 [2, 4, 768], replicated
- norm_average_new: float32 [2, 4, 768], replicated
Inputs may be any that keep to these rules, and one draw needn't show every extreme that they name: deal is a permutation; slots of group g (rows g * 3072 to (g + 1) * 3072 - 1) take arrival rows of the same group. inverse[deal[s]] = s for every slot s. `micro`: each row is a permutation of the packs 0 to 1. `norm_params`: entries 0 and 2 of the second dimension are gains near 1, entries 1 and 3 biases near 0.
All inputs are finite; a program needn't handle non-finite values.
Results may differ from a plain program's by a relative error of at most 0.03.
The roundings to bfloat16 on the way count: a program that leaves them out, or rounds other values in their place, can miss the bound.
Values may be sent and summed in bfloat16 or wider, within the bound.
No kernel may reach another device: no remote copies, remote signals or barrier semaphores. Data moves between devices by JAX's collectives and lax.ppermute only.
A program may use at most 448 MiB of HBM per device.

v0:
```python
import math

import jax
import jax.numpy as jnp
from jax import lax
from jax.sharding import PartitionSpec as P

D = 768
HEAD_DIM = 64
FF = 3072
SEQ_MOST = 1024


norm_eps = 1e-05
rope_base = 1000.0
step_size = 2.0
norm_step = 0.1
keep_rate = 0.5
masked_value = -1e30


def rounded(values):
    return lax.optimization_barrier(values.astype(jnp.bfloat16)).astype(jnp.float32)


def documents(doc_lengths, pack_rows):
    doc_ends = jnp.cumsum(doc_lengths)
    row_ids = jnp.arange(pack_rows, dtype=jnp.int32)
    passed = (row_ids[:, None] >= doc_ends[None, :]).astype(jnp.int32)
    doc_ids = jnp.sum(passed, axis=1)
    doc_starts = jnp.sum(passed * doc_lengths[None, :], axis=1)
    return (doc_ids, (row_ids - doc_starts).astype(jnp.float32))


def rotary(positions, head_width):
    half_width = head_width // 2
    frequency = jnp.exp(
        jnp.arange(half_width, dtype=jnp.float32) * (-2.0 * math.log(rope_base) / head_width)
    )
    angles = positions[:, None] * frequency[None, :]
    cosine = jnp.concatenate([jnp.cos(angles), jnp.cos(angles)], axis=1)[:, None, :]
    sine_table = jnp.concatenate([jnp.sin(angles), jnp.sin(angles)], axis=1)[:, None, :]
    return (cosine, sine_table)


def rotate(values, cosine, sine_table):
    half_width = values.shape[-1] // 2
    turned = jnp.concatenate([-values[..., half_width:], values[..., :half_width]], axis=-1)
    return values * cosine + turned * sine_table


def layer_norm(summed, gain_row, bias_row):
    row_mean = jnp.mean(summed, axis=-1, keepdims=True)
    centred = summed - row_mean
    variance = jnp.mean(centred * centred, axis=-1, keepdims=True)
    inv_std = lax.rsqrt(variance + norm_eps)
    normed = centred * inv_std
    return (normed * gain_row + bias_row, normed, inv_std)


def norm_back(grad_out, normed, inv_std, gain_row):
    grad_norm = grad_out * gain_row
    return inv_std * (
        grad_norm
        - jnp.mean(grad_norm, axis=-1, keepdims=True)
        - normed * jnp.mean(grad_norm * normed, axis=-1, keepdims=True)
    )


def masked_scores(query_block, key_rows, mask_block):
    scores = jnp.einsum(
        "qhd,khd->hqk", query_block, key_rows, preferred_element_type=jnp.float32
    ) * HEAD_DIM ** (-0.5)
    return jnp.where(mask_block[None], scores, masked_value)


def forward_layer(inputs_full, inputs_own, mats, norm_rows, cosine, sine_table, same_doc):
    qkv_mat, proj_mat, gate_mat, down_mat = mats
    row_count = inputs_full.shape[0]
    head_count = qkv_mat.shape[2] // HEAD_DIM
    projected = jnp.einsum("rd,djc->rjc", inputs_full, qkv_mat, preferred_element_type=jnp.float32)
    split_shape = (row_count, head_count, HEAD_DIM)
    queries = rotate(projected[:, 0].reshape(split_shape), cosine, sine_table).astype(jnp.bfloat16)
    key_rows = rotate(projected[:, 1].reshape(split_shape), cosine, sine_table).astype(jnp.bfloat16)
    value_rows = projected[:, 2].reshape(split_shape).astype(jnp.bfloat16)
    block_rows = min(512, row_count)
    attended_parts = []
    log_parts = []
    for offset in range(0, row_count, block_rows):
        scores = masked_scores(
            queries[offset : offset + block_rows], key_rows, same_doc[offset : offset + block_rows]
        )
        row_max = jnp.max(scores, axis=-1, keepdims=True)
        exponent = jnp.exp(scores - row_max)
        totals = jnp.sum(exponent, axis=-1, keepdims=True)
        probs_soft = (exponent / totals).astype(jnp.bfloat16)
        log_parts.append(row_max + jnp.log(totals))
        attended_parts.append(
            jnp.einsum("hqk,khd->qhd", probs_soft, value_rows, preferred_element_type=jnp.float32)
        )
    attended = (
        jnp.concatenate(attended_parts, axis=0)
        .reshape(row_count, head_count * HEAD_DIM)
        .astype(jnp.bfloat16)
    )
    log_sums = jnp.concatenate(log_parts, axis=1)
    piece_rows = attended
    attn_out = lax.psum_scatter(
        jnp.einsum("rc,dc->rd", piece_rows, proj_mat, preferred_element_type=jnp.float32),
        "tensor",
        scatter_dimension=0,
        tiled=True,
    )
    middle, normed_mid, inv_mid = layer_norm(inputs_own + attn_out, norm_rows[0], norm_rows[1])
    middle_full = lax.all_gather(middle.astype(jnp.bfloat16), "tensor", axis=0, tiled=True)
    gate_up = jnp.einsum("rd,djc->rjc", middle_full, gate_mat, preferred_element_type=jnp.float32)
    hidden = (jax.nn.silu(gate_up[:, 0]) * gate_up[:, 1]).astype(jnp.bfloat16)
    piece_rows = hidden
    ffn_out = lax.psum_scatter(
        jnp.einsum("rc,dc->rd", piece_rows, down_mat, preferred_element_type=jnp.float32),
        "tensor",
        scatter_dimension=0,
        tiled=True,
    )
    result, normed_out, inv_out = layer_norm(middle + ffn_out, norm_rows[2], norm_rows[3])
    kept = (
        inputs_full,
        queries,
        key_rows,
        value_rows,
        log_sums,
        attended,
        normed_mid,
        inv_mid,
        middle_full,
        gate_up,
        hidden,
        normed_out,
        inv_out,
    )
    return (kept, result)


def backward_layer(grad_own, mats, norm_rows, kept, cosine, sine_table, same_doc):
    (
        inputs_full,
        queries,
        key_rows,
        value_rows,
        log_sums,
        attended,
        normed_mid,
        inv_mid,
        middle_full,
        gate_up,
        hidden,
        normed_out,
        inv_out,
    ) = kept
    qkv_mat, proj_mat, gate_mat, down_mat = mats
    row_count = inputs_full.shape[0]
    head_count = qkv_mat.shape[2] // HEAD_DIM
    scale = HEAD_DIM ** (-0.5)
    gain_out = jnp.sum(grad_own * normed_out, axis=0)
    bias_out = jnp.sum(grad_own, axis=0)
    grad_sum2 = norm_back(grad_own, normed_out, inv_out, norm_rows[2])
    sum2_full = lax.all_gather(grad_sum2.astype(jnp.bfloat16), "tensor", axis=0, tiled=True)
    down_part = jnp.einsum("rd,rc->dc", sum2_full, hidden, preferred_element_type=jnp.float32)
    grad_hidden = rounded(
        jnp.einsum("rd,dc->rc", sum2_full, down_mat, preferred_element_type=jnp.float32)
    )
    gate_vals = gate_up[:, 0]
    up_vals = gate_up[:, 1]
    sigmoid_vals = jax.nn.sigmoid(gate_vals)
    grad_gate = grad_hidden * up_vals * sigmoid_vals * (1.0 + gate_vals * (1.0 - sigmoid_vals))
    grad_up = grad_hidden * gate_vals * sigmoid_vals
    grad_gate_up = jnp.stack([grad_gate, grad_up], axis=1).astype(jnp.bfloat16)
    gate_part = jnp.einsum(
        "rd,rjc->djc", middle_full, grad_gate_up, preferred_element_type=jnp.float32
    )
    piece_rows = grad_gate_up
    grad_mid = (
        lax.psum_scatter(
            jnp.einsum("rjc,djc->rd", piece_rows, gate_mat, preferred_element_type=jnp.float32),
            "tensor",
            scatter_dimension=0,
            tiled=True,
        )
        + grad_sum2
    )
    gain_mid = jnp.sum(grad_mid * normed_mid, axis=0)
    bias_mid = jnp.sum(grad_mid, axis=0)
    grad_sum1 = norm_back(grad_mid, normed_mid, inv_mid, norm_rows[0])
    sum1_full = lax.all_gather(grad_sum1.astype(jnp.bfloat16), "tensor", axis=0, tiled=True)
    proj_part = jnp.einsum("rd,rc->dc", sum1_full, attended, preferred_element_type=jnp.float32)
    grad_attended = jnp.einsum(
        "rd,dc->rc", sum1_full, proj_mat, preferred_element_type=jnp.float32
    ).astype(jnp.bfloat16)
    grad_attended = grad_attended.reshape(row_count, head_count, HEAD_DIM)
    block_rows = min(512, row_count)
    query_grads = []
    key_grad = jnp.zeros((row_count, head_count, HEAD_DIM), jnp.float32)
    value_grad = jnp.zeros((row_count, head_count, HEAD_DIM), jnp.float32)
    for offset in range(0, row_count, block_rows):
        query_block = queries[offset : offset + block_rows]
        scores = masked_scores(query_block, key_rows, same_doc[offset : offset + block_rows])
        probs_soft = jnp.exp(scores - log_sums[:, offset : offset + block_rows])
        grad_block = grad_attended[offset : offset + block_rows]
        grad_probs = jnp.einsum(
            "qhd,khd->hqk", grad_block, value_rows, preferred_element_type=jnp.float32
        )
        centre = jnp.sum(probs_soft * grad_probs, axis=-1, keepdims=True)
        grad_scores = (probs_soft * (grad_probs - centre)).astype(jnp.bfloat16)
        query_grads.append(
            jnp.einsum("hqk,khd->qhd", grad_scores, key_rows, preferred_element_type=jnp.float32)
            * scale
        )
        key_grad = (
            key_grad
            + jnp.einsum(
                "hqk,qhd->khd", grad_scores, query_block, preferred_element_type=jnp.float32
            )
            * scale
        )
        value_grad = value_grad + jnp.einsum(
            "hqk,qhd->khd",
            probs_soft.astype(jnp.bfloat16),
            grad_block,
            preferred_element_type=jnp.float32,
        )
    query_grad = rotate(jnp.concatenate(query_grads, axis=0), cosine, -sine_table)
    key_grad = rotate(key_grad, cosine, -sine_table)
    grad_projected = (
        jnp.stack([query_grad, key_grad, value_grad], axis=1)
        .reshape(row_count, 3, head_count * HEAD_DIM)
        .astype(jnp.bfloat16)
    )
    qkv_part = jnp.einsum(
        "rd,rjc->djc", inputs_full, grad_projected, preferred_element_type=jnp.float32
    )
    piece_rows = grad_projected
    grad_input = (
        lax.psum_scatter(
            jnp.einsum("rjc,djc->rd", piece_rows, qkv_mat, preferred_element_type=jnp.float32),
            "tensor",
            scatter_dimension=0,
            tiled=True,
        )
        + grad_sum1
    )
    norm_part = jnp.stack([gain_mid, bias_mid, gain_out, bias_out], axis=0)
    return ((qkv_part, proj_part, gate_part, down_part), norm_part, grad_input)


def update(weight, gradient, moment, average, rate):
    moment_new = keep_rate * moment + gradient
    weight_new = weight - rate * (gradient + keep_rate * moment_new)
    average_new = keep_rate * average + (1.0 - keep_rate) * weight_new
    return (gradient, weight_new, moment_new, average_new)


def per_device(
    hidden_in,
    cotangent,
    lengths,
    deal,
    inverse,
    micro,
    qkv_weight,
    proj_weight,
    gate_up_weight,
    down_weight,
    norm_params,
    qkv_momentum,
    proj_momentum,
    gate_up_momentum,
    down_momentum,
    norm_momentum,
    qkv_average,
    proj_average,
    gate_up_average,
    down_average,
    norm_average,
):
    layers = qkv_weight.shape[0]
    batches = micro.shape[1]
    width = hidden_in.shape[1]
    local_rows = hidden_in.shape[0]
    group_rows = deal.shape[0]
    pack_rows = group_rows // batches
    splits = lax.axis_size("tensor")
    own_rows = pack_rows // splits
    tensor_rank = lax.axis_index("tensor")
    group_base = lax.axis_index("dp") * group_rows
    arrivals, arrival_grads = (
        lax.all_gather(hidden_in, "tensor", axis=0, tiled=True),
        lax.all_gather(cotangent, "tensor", axis=0, tiled=True),
    )
    local_deal = deal - group_base
    dealt_in = arrivals[local_deal]
    dealt_grad = arrival_grads[local_deal]
    shard_sums = [
        (
            jnp.zeros(qkv_weight.shape[1:], jnp.float32),
            jnp.zeros(proj_weight.shape[1:], jnp.float32),
            jnp.zeros(gate_up_weight.shape[1:], jnp.float32),
            jnp.zeros(down_weight.shape[1:], jnp.float32),
        )
        for layer_idx in range(layers)
    ]
    norm_sums = [jnp.zeros(norm_params.shape[1:], jnp.float32) for layer_idx in range(layers)]
    out_list = []
    back_list = []
    for batch_idx in range(batches):
        pack_slot = micro[0, batch_idx]
        pack_in = lax.dynamic_slice_in_dim(dealt_in, pack_slot * pack_rows, pack_rows, 0)
        pack_cot = lax.dynamic_slice_in_dim(dealt_grad, pack_slot * pack_rows, pack_rows, 0)
        inputs_own = lax.dynamic_slice_in_dim(pack_in, tensor_rank * own_rows, own_rows, 0).astype(
            jnp.float32
        )
        grad_own = lax.dynamic_slice_in_dim(pack_cot, tensor_rank * own_rows, own_rows, 0).astype(
            jnp.float32
        )
        doc_ids, positions = documents(lengths[0, batch_idx], pack_rows)
        same_doc = doc_ids[:, None] == doc_ids[None, :]
        cosine, sine_table = rotary(positions, HEAD_DIM)
        stash = []
        inputs_full = pack_in
        for layer_idx in range(layers):
            mats = (
                lax.all_gather(
                    qkv_weight[layer_idx].astype(jnp.bfloat16), "dp", axis=0, tiled=True
                ),
                lax.all_gather(
                    proj_weight[layer_idx].astype(jnp.bfloat16), "dp", axis=0, tiled=True
                ),
                lax.all_gather(
                    gate_up_weight[layer_idx].astype(jnp.bfloat16), "dp", axis=0, tiled=True
                ),
                lax.all_gather(
                    down_weight[layer_idx].astype(jnp.bfloat16), "dp", axis=0, tiled=True
                ),
            )
            if layer_idx > 0:
                inputs_full = lax.all_gather(
                    inputs_own.astype(jnp.bfloat16), "tensor", axis=0, tiled=True
                )
            kept, inputs_own = forward_layer(
                inputs_full, inputs_own, mats, norm_params[layer_idx], cosine, sine_table, same_doc
            )
            stash.append((mats, kept))
        out_list.append(inputs_own)
        for layer_idx in range(layers - 1, -1, -1):
            mats, kept = stash[layer_idx]
            weight_parts, norm_part, grad_own = backward_layer(
                grad_own, mats, norm_params[layer_idx], kept, cosine, sine_table, same_doc
            )
            norm_sums[layer_idx] = norm_sums[layer_idx] + norm_part
            qkv_part, proj_part, gate_part, down_part = weight_parts
            qkv_share, proj_share, gate_share, down_share = (
                lax.psum_scatter(qkv_part, "dp", scatter_dimension=0, tiled=True),
                lax.psum_scatter(proj_part, "dp", scatter_dimension=0, tiled=True),
                lax.psum_scatter(gate_part, "dp", scatter_dimension=0, tiled=True),
                lax.psum_scatter(down_part, "dp", scatter_dimension=0, tiled=True),
            )
            before = shard_sums[layer_idx]
            shard_sums[layer_idx] = (
                before[0] + qkv_share,
                before[1] + proj_share,
                before[2] + gate_share,
                before[3] + down_share,
            )
        back_list.append(grad_own)
    norm_total = lax.psum(jnp.stack(norm_sums, axis=0), ("dp", "tensor"))
    out_full, back_full = (
        lax.all_gather(jnp.stack(out_list, axis=0), "tensor", axis=1, tiled=True),
        lax.all_gather(jnp.stack(back_list, axis=0), "tensor", axis=1, tiled=True),
    )
    arrival_ids = tensor_rank * local_rows + jnp.arange(local_rows, dtype=jnp.int32)
    slot_ids = inverse[arrival_ids] - group_base
    pack_ids = slot_ids // pack_rows
    within = slot_ids % pack_rows
    matches = (micro[0][None, :] == pack_ids[:, None]).astype(jnp.int32)
    batch_ids = jnp.sum(matches * jnp.arange(batches, dtype=jnp.int32)[None, :], axis=1)
    flat_ids = batch_ids * pack_rows + within
    block_out = out_full.reshape(batches * pack_rows, width)[flat_ids]
    input_grad = back_full.reshape(batches * pack_rows, width)[flat_ids]
    total_tokens = local_rows * lax.axis_size("dp") * splits
    proj_fan = max(1, D * 8 // SEQ_MOST)
    qkv_grad = jnp.stack([shard_sums[idx][0] for idx in range(layers)], axis=0)
    proj_grad = jnp.stack([shard_sums[idx][1] for idx in range(layers)], axis=0)
    gate_grad = jnp.stack([shard_sums[idx][2] for idx in range(layers)], axis=0)
    down_grad = jnp.stack([shard_sums[idx][3] for idx in range(layers)], axis=0)
    qkv_state = update(
        qkv_weight, qkv_grad, qkv_momentum, qkv_average, step_size / math.sqrt(total_tokens * D)
    )
    proj_state = update(
        proj_weight,
        proj_grad,
        proj_momentum,
        proj_average,
        step_size / math.sqrt(total_tokens * proj_fan),
    )
    gate_state = update(
        gate_up_weight,
        gate_grad,
        gate_up_momentum,
        gate_up_average,
        step_size / math.sqrt(total_tokens * D),
    )
    down_state = update(
        down_weight,
        down_grad,
        down_momentum,
        down_average,
        step_size / math.sqrt(total_tokens * FF),
    )
    norm_state = update(
        norm_params, norm_total, norm_momentum, norm_average, norm_step / math.sqrt(total_tokens)
    )
    return (
        block_out,
        input_grad,
        qkv_state[0],
        qkv_state[1],
        qkv_state[2],
        qkv_state[3],
        proj_state[0],
        proj_state[1],
        proj_state[2],
        proj_state[3],
        gate_state[0],
        gate_state[1],
        gate_state[2],
        gate_state[3],
        down_state[0],
        down_state[1],
        down_state[2],
        down_state[3],
        norm_state[0],
        norm_state[1],
        norm_state[2],
        norm_state[3],
    )


def solution(mesh):
    placed = (
        P(("dp", "tensor"), None),
        P(("dp", "tensor"), None),
        P("dp", None, None),
        P("dp"),
        P("dp"),
        P("dp", None),
        P(None, "dp", None, "tensor"),
        P(None, "dp", "tensor"),
        P(None, "dp", None, "tensor"),
        P(None, "dp", "tensor"),
        P(),
        P(None, "dp", None, "tensor"),
        P(None, "dp", "tensor"),
        P(None, "dp", None, "tensor"),
        P(None, "dp", "tensor"),
        P(),
        P(None, "dp", None, "tensor"),
        P(None, "dp", "tensor"),
        P(None, "dp", None, "tensor"),
        P(None, "dp", "tensor"),
        P(),
    )
    return jax.shard_map(
        per_device,
        mesh=mesh,
        in_specs=placed,
        out_specs=(
            P(("dp", "tensor"), None),
            P(("dp", "tensor"), None),
            P(None, "dp", None, "tensor"),
            P(None, "dp", None, "tensor"),
            P(None, "dp", None, "tensor"),
            P(None, "dp", None, "tensor"),
            P(None, "dp", "tensor"),
            P(None, "dp", "tensor"),
            P(None, "dp", "tensor"),
            P(None, "dp", "tensor"),
            P(None, "dp", None, "tensor"),
            P(None, "dp", None, "tensor"),
            P(None, "dp", None, "tensor"),
            P(None, "dp", None, "tensor"),
            P(None, "dp", "tensor"),
            P(None, "dp", "tensor"),
            P(None, "dp", "tensor"),
            P(None, "dp", "tensor"),
            P(),
            P(),
            P(),
            P(),
        ),
        check_vma=False,
    )
```

profile of v0, /device:TPU:0, one launch (start us, length us, event | category | flops | bytes accessed | tf_op | source)
XLA Modules:
  0.0 2352.0 jit_solution(17483476352754336587)
XLA Ops:
  13.8 38.8 %all-gather = bf16[1,768,3,192]{3,2,0,1:T(4,128)(2,1)S(1)} all-gather(bf16[1,96,3,192]{3,2,0,1:T(4,128)(2,1)S(1)} %get-tuple-element.298), channel_id=2, replica_groups=mesh['dp'=8,'tensor'=4] {'dp'}, dimensions={1}, use_global_device_ids=true | all-gather | bytes 995328 | tf_op jit(solution)/shard_map/all_gather | solution.py:331
  55.9 31.0 %all-gather.1 = bf16[1,768,192]{2,1,0:T(8,128)(2,1)S(1)} all-gather(bf16[1,96,192]{2,1,0:T(8,128)(2,1)S(1)} %get-tuple-element.310), channel_id=3, replica_groups=mesh['dp'=8,'tensor'=4] {'dp'}, dimensions={1}, use_global_device_ids=true | all-gather | bytes 331776 | tf_op jit(solution)/shard_map/all_gather | solution.py:334
  196.3 50.5 %reduce-scatter.33.cloned.1.call-done = f32[384,768]{1,0:T(8,128)} async-done(((f32[1536,768]{1,0:T(8,128)}), f32[384,768]{1,0:T(8,128)}) %reduce-scatter.33.cloned.1.call-update) | async-done | bytes 1179664 | tf_op jit(solution)/shard_map/reduce_scatter | solution.py:108
  286.9 31.9 %all-gather.69.cloned.1.call-done = bf16[1,768,768]{2,1,0:T(8,128)(2,1)} async-done(((bf16[1,96,768]{2,1,0:T(8,128)(2,1)}), bf16[1,768,768]{2,1,0:T(8,128)(2,1)}) %all-gather.69.cloned.1.call-update) | async-done | bytes 1179664 | tf_op jit(solution)/shard_map/all_gather | solution.py:340
  325.9 45.4 %reduce-scatter.27.cloned.1.call-done = f32[384,768]{1,0:T(8,128)} async-done(((f32[1536,768]{1,0:T(8,128)}), f32[384,768]{1,0:T(8,128)}) %reduce-scatter.27.cloned.1.call-update) | async-done | bytes 1179664 | tf_op jit(solution)/shard_map/reduce_scatter | solution.py:119
  377.7 38.6 %all-gather.4 = bf16[1,768,3,192]{3,2,0,1:T(4,128)(2,1)} all-gather(bf16[1,96,3,192]{3,2,0,1:T(4,128)(2,1)S(1)} %copy-done.174), channel_id=6, replica_groups=mesh['dp'=8,'tensor'=4] {'dp'}, dimensions={1}, use_global_device_ids=true | all-gather | bytes 995328 | tf_op jit(solution)/shard_map/all_gather | solution.py:331
  419.8 31.0 %all-gather.5 = bf16[1,768,192]{2,1,0:T(8,128)(2,1)S(1)} all-gather(bf16[1,96,192]{2,1,0:T(8,128)(2,1)S(1)} %copy-done.205), channel_id=7, replica_groups=mesh['dp'=8,'tensor'=4] {'dp'}, dimensions={1}, use_global_device_ids=true | all-gather | bytes 331776 | tf_op jit(solution)/shard_map/all_gather | solution.py:334
  517.1 47.1 %reduce-scatter.29.cloned.1.call-done = f32[384,768]{1,0:T(8,128)} async-done(((f32[1536,768]{1,0:T(8,128)}), f32[384,768]{1,0:T(8,128)}) %reduce-scatter.29.cloned.1.call-update) | async-done | bytes 1179664 | tf_op jit(solution)/shard_map/reduce_scatter | solution.py:108
  682.5 31.5 %all-gather.73.cloned.1.call-done = bf16[1,768,768]{2,1,0:T(8,128)(2,1)} async-done(((bf16[1,96,768]{2,1,0:T(8,128)(2,1)}), bf16[1,768,768]{2,1,0:T(8,128)(2,1)}) %all-gather.73.cloned.1.call-update) | async-done | bytes 1179664 | tf_op jit(solution)/shard_map/all_gather | solution.py:340
  720.3 42.4 %reduce-scatter.37.cloned.1.call-done = f32[384,768]{1,0:T(8,128)} async-done(((f32[1536,768]{1,0:T(8,128)}), f32[384,768]{1,0:T(8,128)}) %reduce-scatter.37.cloned.1.call-update) | async-done | bytes 1179664 | tf_op jit(solution)/shard_map/reduce_scatter | solution.py:108
  765.3 47.9 %reduce-scatter.31.cloned.1.call-done = f32[384,768]{1,0:T(8,128)} async-done(((f32[1536,768]{1,0:T(8,128)}), f32[384,768]{1,0:T(8,128)}) %reduce-scatter.31.cloned.1.call-update) | async-done | bytes 1179664 | tf_op jit(solution)/shard_map/reduce_scatter | solution.py:119
  900.3 29.9 %reduce-scatter.39.cloned.1.call-done = f32[384,768]{1,0:T(8,128)} async-done(((f32[1536,768]{1,0:T(8,128)}), f32[384,768]{1,0:T(8,128)}) %reduce-scatter.39.cloned.1.call-update) | async-done | bytes 1179664 | tf_op jit(solution)/shard_map/reduce_scatter | solution.py:119
  1030.3 46.3 %reduce-scatter.49.cloned.1.call-done = f32[384,768]{1,0:T(8,128)} async-done(((f32[1536,768]{1,0:T(8,128)}), f32[384,768]{1,0:T(8,128)}) %reduce-scatter.49.cloned.1.call-update) | async-done | bytes 1179664 | tf_op jit(solution)/shard_map/reduce_scatter | solution.py:183
  1252.9 41.7 %reduce-scatter.51.cloned.1.call-done = f32[384,768]{1,0:T(8,128)} async-done(((f32[1536,768]{1,0:T(8,128)}), f32[384,768]{1,0:T(8,128)}) %reduce-scatter.51.cloned.1.call-update) | async-done | bytes 1179664 | tf_op jit(solution)/shard_map/reduce_scatter | solution.py:243
  1366.9 33.6 %reduce-scatter.45.cloned.1.call-done = f32[384,768]{1,0:T(8,128)} async-done(((f32[1536,768]{1,0:T(8,128)}), f32[384,768]{1,0:T(8,128)}) %reduce-scatter.45.cloned.1.call-update) | async-done | bytes 1179664 | tf_op jit(solution)/shard_map/reduce_scatter | solution.py:183
  1405.5 45.4 %reduce-scatter.53.cloned.1.call-done = f32[384,768]{1,0:T(8,128)} async-done(((f32[1536,768]{1,0:T(8,128)}), f32[384,768]{1,0:T(8,128)}) %reduce-scatter.53.cloned.1.call-update) | async-done | bytes 1179664 | tf_op jit(solution)/shard_map/reduce_scatter | solution.py:183
  1734.8 52.9 %reduce-scatter.71.cloned.1.call-done = f32[96,768]{1,0:T(8,128)} async-done(((f32[768,768]{1,0:T(8,128)}), f32[96,768]{1,0:T(8,128)}) %reduce-scatter.71.cloned.1.call-update) | async-done | bytes 294928 | tf_op jit(solution)/shard_map/reduce_scatter | solution.py:364
  1787.7 72.5 %reduce-scatter.69.cloned.1.call-done = f32[96,768]{1,0:T(8,128)} async-done(((f32[768,768]{1,0:T(8,128)}), f32[96,768]{1,0:T(8,128)}) %reduce-scatter.69.cloned.1.call-update) | async-done | bytes 294928 | tf_op jit(solution)/shard_map/reduce_scatter | solution.py:364
  1863.1 95.5 %reduce-scatter.67.cloned.1.call-done = f32[96,2,768]{2,0,1:T(8,128)} async-done(((f32[768,2,768]{2,0,1:T(8,128)}), f32[96,2,768]{2,0,1:T(8,128)}) %reduce-scatter.67.cloned.1.call-update) | async-done | bytes 589840 | tf_op jit(solution)/shard_map/reduce_scatter | solution.py:363
  1958.6 99.0 %reduce-scatter.65.cloned.1.call-done = f32[96,2,768]{2,0,1:T(8,128)} async-done(((f32[768,2,768]{2,0,1:T(8,128)}), f32[96,2,768]{2,0,1:T(8,128)}) %reduce-scatter.65.cloned.1.call-update) | async-done | bytes 589840 | tf_op jit(solution)/shard_map/reduce_scatter | solution.py:363
  2067.7 40.4 %psum.7 = f32[2,4,768]{2,1,0:T(4,128)S(1)} all-reduce(f32[2,4,768]{2,1,0:T(4,128)S(1)} %pad_maximum_fusion.50), channel_id=1, replica_groups=mesh['dp'=8,'tensor'=4] {'dp','tensor'}, use_global_device_ids=true, to_apply=%region_123.124 | all-reduce | flops 6144 | bytes 49152 | tf_op jit(solution)/shard_map/psum | solution.py:374
  2123.9 65.5 %reduce-scatter.61.cloned.1.call-done = f32[96,192]{1,0:T(8,128)} async-done(((f32[768,192]{1,0:T(8,128)}), f32[96,192]{1,0:T(8,128)}) %reduce-scatter.61.cloned.1.call-update) | async-done | bytes 73744 | tf_op jit(solution)/shard_map/reduce_scatter | solution.py:362
  2191.2 70.5 %reduce-scatter.59.cloned.1.call-done = f32[96,3,192]{2,0,1:T(8,128)} async-done(((f32[768,3,192]{2,0,1:T(8,128)}), f32[96,3,192]{2,0,1:T(8,128)}) %reduce-scatter.59.cloned.1.call-update) | async-done | bytes 221200 | tf_op jit(solution)/shard_map/reduce_scatter | solution.py:361
  2261.8 72.5 %reduce-scatter.57.cloned.1.call-done = f32[96,3,192]{2,0,1:T(8,128)} async-done(((f32[768,3,192]{2,0,1:T(8,128)}), f32[96,3,192]{2,0,1:T(8,128)}) %reduce-scatter.57.cloned.1.call-update) | async-done | bytes 221200 | tf_op jit(solution)/shard_map/reduce_scatter | solution.py:361
  (1203 shorter events, 1128.1 us)
Async XLA Ops:
  8.8 187.5 %reduce-scatter.25.cloned.1.call-start = ((), (), s32[]{:S(2)}) async-start(), calls=%async_computation.25 | async-start | bytes 5898240 | tf_op jit(solution)/shard_map/reduce_scatter | solution.py:108
  251.7 119.6 %reduce-scatter.27.cloned.1.call-start = ((), (), s32[]{:S(2)}) async-start(), calls=%async_computation.27 | async-start | bytes 5898240 | tf_op jit(solution)/shard_map/reduce_scatter | solution.py:119
  325.0 125.8 %all-gather.39.cloned.1.call-start = ((), (), s32[]{:S(2)}) async-start(), calls=%async_computation.33 | async-start | bytes 2949120 | tf_op jit(solution)/shard_map/all_gather | solution.py:115
  377.6 136.2 %reduce-scatter.35.cloned.1.call-start = ((), (), s32[]{:S(2)}) async-start(), calls=%async_computation.34 | async-start | bytes 5898240 | tf_op jit(solution)/shard_map/reduce_scatter | solution.py:119
  570.9 143.1 %all-gather.73.cloned.1.call-start = ((), (), s32[]{:S(2)}) async-start(), calls=%async_computation.61 | async-start | bytes 1327104 | tf_op jit(solution)/shard_map/all_gather | solution.py:340
  571.7 191.0 %reduce-scatter.37.cloned.1.call-start = ((), (), s32[]{:S(2)}) async-start(), calls=%async_computation.36 | async-start | bytes 5898240 | tf_op jit(solution)/shard_map/reduce_scatter | solution.py:108
  630.3 182.8 %reduce-scatter.31.cloned.1.call-start = ((), (), s32[]{:S(2)}) async-start(), calls=%async_computation.31 | async-start | bytes 5898240 | tf_op jit(solution)/shard_map/reduce_scatter | solution.py:119
  720.3 120.3 %all-gather.43.cloned.1.call-start = ((), (), s32[]{:S(2)}) async-start(), calls=%async_computation.37 | async-start | bytes 2949120 | tf_op jit(solution)/shard_map/all_gather | solution.py:115
  817.1 113.0 %reduce-scatter.39.cloned.1.call-start = ((), (), s32[]{:S(2)}) async-start(), calls=%async_computation.38 | async-start | bytes 5898240 | tf_op jit(solution)/shard_map/reduce_scatter | solution.py:119
  1083.5 163.2 %reduce-scatter.43.cloned.1.call-start = ((), (), s32[]{:S(2)}) async-start(), calls=%async_computation.44 | async-start | bytes 5898240 | tf_op jit(solution)/shard_map/reduce_scatter | solution.py:243
  1175.6 119.0 %reduce-scatter.51.cloned.1.call-start = ((), (), s32[]{:S(2)}) async-start(), calls=%async_computation.52 | async-start | bytes 5898240 | tf_op jit(solution)/shard_map/reduce_scatter | solution.py:243
  1340.8 110.2 %reduce-scatter.53.cloned.1.call-start = ((), (), s32[]{:S(2)}) async-start(), calls=%async_computation.54 | async-start | bytes 5898240 | tf_op jit(solution)/shard_map/reduce_scatter | solution.py:183
  1366.8 114.7 %all-gather.63.cloned.1.call-start = ((), (), s32[]{:S(2)}) async-start(), calls=%async_computation.55 | async-start | bytes 2949120 | tf_op jit(solution)/shard_map/all_gather | solution.py:194
  1459.5 240.5 %reduce-scatter.55.cloned.1.call-start = ((), (), s32[]{:S(2)}) async-start(), calls=%async_computation.56 | async-start | bytes 5898240 | tf_op jit(solution)/shard_map/reduce_scatter | solution.py:243
  1553.1 161.1 %reduce-scatter.47.cloned.1.call-start = ((), (), s32[]{:S(2)}) async-start(), calls=%async_computation.48 | async-start | bytes 5898240 | tf_op jit(solution)/shard_map/reduce_scatter | solution.py:243
  1625.0 162.8 %reduce-scatter.71.cloned.1.call-start = ((), (), s32[]{:S(2)}) async-start(), calls=%async_computation.69 | async-start | bytes 2654208 | tf_op jit(solution)/shard_map/reduce_scatter | solution.py:364
  1634.5 225.7 %reduce-scatter.69.cloned.1.call-start = ((), (), s32[]{:S(2)}) async-start(), calls=%async_computation.68 | async-start | bytes 2654208 | tf_op jit(solution)/shard_map/reduce_scatter | solution.py:364
  1644.1 314.6 %reduce-scatter.67.cloned.1.call-start = ((), (), s32[]{:S(2)}) async-start(), calls=%async_computation.67 | async-start | bytes 5308416 | tf_op jit(solution)/shard_map/reduce_scatter | solution.py:363
  1657.6 400.0 %reduce-scatter.65.cloned.1.call-start = ((), (), s32[]{:S(2)}) async-start(), calls=%async_computation.66 | async-start | bytes 5308416 | tf_op jit(solution)/shard_map/reduce_scatter | solution.py:363
  1671.4 452.4 %reduce-scatter.63.cloned.1.call-start = ((), (), s32[]{:S(2)}) async-start(), calls=%async_computation.65 | async-start | bytes 884736 | tf_op jit(solution)/shard_map/reduce_scatter | solution.py:362
  1676.6 512.8 %reduce-scatter.61.cloned.1.call-start = ((), (), s32[]{:S(2)}) async-start(), calls=%async_computation.64 | async-start | bytes 884736 | tf_op jit(solution)/shard_map/reduce_scatter | solution.py:362
  1681.1 580.7 %reduce-scatter.59.cloned.1.call-start = ((), (), s32[]{:S(2)}) async-start(), calls=%async_computation.63 | async-start | bytes 2654208 | tf_op jit(solution)/shard_map/reduce_scatter | solution.py:361
  1689.5 644.8 %reduce-scatter.57.cloned.1.call-start = ((), (), s32[]{:S(2)}) async-start(), calls=%async_computation.62 | async-start | bytes 2654208 | tf_op jit(solution)/shard_map/reduce_scatter | solution.py:361
  1699.8 637.1 %all-gather.65.cloned.1.call-start = ((), (), s32[]{:S(2)}) async-start(), calls=%async_computation.57 | async-start | bytes 11796480 | tf_op jit(solution)/shard_map/all_gather | solution.py:377
  (381 other events, 9564.9 us)
Sparse Core Ops, SparseCore 0:
  10.4 40.1 all-gather.30
  149.0 47.2 reduce-scatter.24
  198.8 47.9 reduce-scatter.32
  466.4 47.4 reduce-scatter.34
  516.3 47.9 reduce-scatter.28
  816.5 24.0 all-gather.42
  842.1 37.4 all-gather.46
  882.1 47.9 reduce-scatter.38
  978.3 47.9 reduce-scatter.40
  1028.6 47.9 reduce-scatter.48
  1299.8 24.0 all-gather.52
  1325.9 24.0 all-gather.60
  1352.5 47.9 reduce-scatter.44
  1402.9 47.9 reduce-scatter.52
  1625.1 64.5 all-gather.44
  1717.4 64.2 all-gather.64
Sparse Core Ops, SparseCore 1:
  193.4 51.0 all-gather.66
  277.4 41.4 all-gather.68
  325.1 46.2 reduce-scatter.26
  374.7 23.9 all-gather.38
  567.6 23.9 all-gather.40
  593.6 51.7 all-gather.70
  672.6 41.4 all-gather.72
  716.5 46.1 reduce-scatter.36
  765.2 47.8 reduce-scatter.30
  963.6 24.0 all-gather.56
  1175.6 47.7 reduce-scatter.42
  1246.7 47.8 reduce-scatter.50
  1457.5 23.9 all-gather.62
  1483.6 23.9 all-gather.54
  1553.2 47.8 reduce-scatter.54
  1621.9 92.3 reduce-scatter.46
  1717.6 70.0 reduce-scatter.70
  1791.2 68.9 reduce-scatter.68
  1863.7 94.8 reduce-scatter.66
  1962.3 95.3 reduce-scatter.64
  2060.9 62.9 reduce-scatter.62
  2127.0 62.3 reduce-scatter.60
  2192.7 69.0 reduce-scatter.58
  2265.3 68.9 reduce-scatter.56
  (6 shorter events, 141.8 us)
where the time goes:
time: 2360 us; the launch traced here: 2350 us
  waiting for transfers between devices  1320 us (56%)
  matrix products  421 us (18%)
  other arithmetic  237 us (10%)
  blocking collectives  180 us (8%)
  local copies, waits for them, and re-layouts  169 us (7%)
    reduce_scatter x2, waiting for transfers between devices, per_device(): lax.psum_scatter(gate_part, 'dp', scatter_dimension=0, tiled=True)  194 us
    reduce_scatter x4, waiting for transfers between devices, backward_layer(): lax.psum_scatter(jnp.einsum('rjc,djc->rd', piece_rows, gate_mat, preferre...  147 us
    reduce_scatter x4, waiting for transfers between devices, forward_layer(): lax.psum_scatter(jnp.einsum('rc,dc->rd', piece_rows, proj_mat, preferred_...  143 us
    reduce_scatter x2, waiting for transfers between devices, per_device(): lax.psum_scatter(qkv_part, 'dp', scatter_dimension=0, tiled=True)  143 us
    reduce_scatter x4, waiting for transfers between devices, forward_layer(): lax.psum_scatter(jnp.einsum('rc,dc->rd', piece_rows, down_mat, preferred_...  129 us
    reduce_scatter x2, waiting for transfers between devices, per_device(): lax.psum_scatter(down_part, 'dp', scatter_dimension=0, tiled=True)  125 us
    unnamed x724, local copies, waits for them, and re-layouts  89.5 us
    reduce_scatter x2, waiting for transfers between devices, per_device(): lax.psum_scatter(proj_part, 'dp', scatter_dimension=0, tiled=True)  80.5 us
  transfers between devices with their start and end apart: 46, of which 36 were waited for; matrix products, arithmetic and copies ran while one was open for 28% of the time, Pallas kernels for 0%

commit v1 on v0

v1 whole, which is shorter than its diff:
```python
import functools
import math

import jax
import jax.numpy as jnp
from jax import lax
from jax.experimental import pallas as pl
from jax.experimental.pallas import tpu as pltpu
from jax.sharding import Mesh, PartitionSpec as P

D = 768
HEAD_DIM = 64
FF = 3072
SEQ_MOST = 1024

norm_eps = 1e-05
rope_base = 1000.0
step_size = 2.0
norm_step = 0.1
keep_rate = 0.5
SCALE2 = HEAD_DIM ** (-0.5) * math.log2(math.e)
NT = (((1,), (1,)), ((), ()))
NN = (((1,), (0,)), ((), ()))
TN = (((0,), (0,)), ((), ()))


def mm(a, b, dims):
    return lax.dot_general(a, b, dims, preferred_element_type=jnp.float32)


def attn_fwd_body(BQ, BK, lo_ref, hi_ref, q_ref, k_ref, v_ref, dq_ref, dk_ref, o_ref, lse_ref):
    R = q_ref.shape[0]
    lane = lax.broadcasted_iota(jnp.int32, (BQ, 128), 1)
    first = lane < HEAD_DIM
    zero = jnp.zeros((BQ, 128), jnp.bfloat16)

    def q_block(i, _):
        rows = pl.ds(pl.multiple_of(i * BQ, BQ), BQ)
        q = q_ref[rows, :]
        qs = (jnp.where(first, q, zero), jnp.where(first, zero, q))
        dq = dq_ref[rows, :]

        def kv_block(j, carry):
            cols = pl.ds(pl.multiple_of(j * BK, BK), BK)
            k = k_ref[cols, :]
            v = v_ref[cols, :]
            same = dq == dk_ref[:, cols]
            out = []
            for h in range(2):
                m, l, acc = carry[h]
                s = mm(qs[h], k, NT) * SCALE2
                s = jnp.where(same, s, -1e30)
                m_new = jnp.maximum(m, jnp.max(s, axis=1, keepdims=True))
                alpha = jnp.exp2(m - m_new)
                p = jnp.exp2(s - m_new)
                l = alpha * l + jnp.sum(p, axis=1, keepdims=True)
                acc = alpha * acc + mm(p.astype(jnp.bfloat16), v, NN)
                out.append((m_new, l, acc))
            return tuple(out)

        start = tuple(
            (jnp.full((BQ, 1), -2e30, jnp.float32), jnp.zeros((BQ, 1), jnp.float32), jnp.zeros((BQ, 128), jnp.float32))
            for h in range(2)
        )
        (m0, l0, a0), (m1, l1, a1) = lax.fori_loop(lo_ref[i], hi_ref[i], kv_block, start)
        o_ref[rows, :] = jnp.where(first, a0 / l0, a1 / l1).astype(jnp.bfloat16)
        lse_ref[rows, :] = jnp.where(first, m0 + jnp.log2(l0), m1 + jnp.log2(l1))
        return 0

    lax.fori_loop(0, R // BQ, q_block, 0)


def attn_fwd(lo, hi, q, k, v, dq, dk, BQ=256, BK=256):
    R, C = q.shape
    pairs = C // 128
    blk = pl.BlockSpec((R, 128), lambda p, *_: (0, p))
    return pl.pallas_call(
        functools.partial(attn_fwd_body, BQ, BK),
        out_shape=(jax.ShapeDtypeStruct((R, C), jnp.bfloat16), jax.ShapeDtypeStruct((R, C), jnp.float32)),
        grid_spec=pltpu.PrefetchScalarGridSpec(
            num_scalar_prefetch=2, grid=(pairs,),
            in_specs=[blk, blk, blk, pl.BlockSpec((R, 1), lambda p, *_: (0, 0)), pl.BlockSpec((1, R), lambda p, *_: (0, 0))],
            out_specs=[blk, blk]),
        cost_estimate=pl.CostEstimate(flops=pairs * 2 * R * R * 64 * 4, bytes_accessed=R * C * 12, transcendentals=pairs * 2 * R * R),
        name="attn_fwd",
    )(lo, hi, q, k, v, dq, dk)


def attn_bwd_body(BQ, BK, mode, lo_ref, hi_ref, q_ref, k_ref, v_ref, do_ref, o_ref, lse_ref, dq_ref, dk_ref,
                  gq_ref, gk_ref, gv_ref, gq_s, lse_s, delta_s):
    R = q_ref.shape[0]
    nq = R // BQ
    scale = HEAD_DIM ** (-0.5)
    gk_ref[...] = jnp.zeros((R, 128), jnp.float32)
    gv_ref[...] = jnp.zeros((R, 128), jnp.float32)
    fq = lax.broadcasted_iota(jnp.int32, (BQ, 128), 1) < HEAD_DIM
    fk = lax.broadcasted_iota(jnp.int32, (BK, 128), 1) < HEAD_DIM
    zq = jnp.zeros((BQ, 128), jnp.bfloat16)
    zk = jnp.zeros((BK, 128), jnp.bfloat16)

    def q_block(i, _):
        rows = pl.ds(pl.multiple_of(i * BQ, BQ), BQ)
        q = q_ref[rows, :]
        do = do_ref[rows, :]
        prod = do.astype(jnp.float32) * o_ref[rows, :].astype(jnp.float32)
        lse_t = lse_ref[rows, :].T
        prod_t = prod.T
        qs = (jnp.where(fq, q, zq), jnp.where(fq, zq, q))
        dos = (jnp.where(fq, do, zq), jnp.where(fq, zq, do))
        lses = (lse_t[0:1, :], lse_t[64:65, :])
        deltas = (jnp.sum(prod_t[:64, :], axis=0, keepdims=True), jnp.sum(prod_t[64:, :], axis=0, keepdims=True))
        dq = dq_ref[:, rows]

        def kv_block(j, acc):
            cols = pl.ds(pl.multiple_of(j * BK, BK), BK)
            k = k_ref[cols, :]
            v = v_ref[cols, :]
            same = dk_ref[cols, :] == dq
            gk = gk_ref[cols, :]
            gv = gv_ref[cols, :]
            ks = (jnp.where(fk, k, zk), jnp.where(fk, zk, k))
            for h in range(2):
                s = mm(k, qs[h], NT) * SCALE2
                p = jnp.exp2(jnp.where(same, s - lses[h], -1e30))
                dp = mm(v, dos[h], NT)
                ds = (p * (dp - deltas[h])).astype(jnp.bfloat16)
                gv = gv + mm(p.astype(jnp.bfloat16), dos[h], NN)
                gk = gk + mm(ds, qs[h], NN)
                acc = acc + mm(ds, ks[h], TN)
            gk_ref[cols, :] = gk
            gv_ref[cols, :] = gv
            return acc

        gq_ref[rows, :] = lax.fori_loop(lo_ref[i], hi_ref[i], kv_block, jnp.zeros((BQ, 128), jnp.float32)) * scale
        return 0

    lax.fori_loop(0, nq, q_block, 0)
    gk_ref[...] = gk_ref[...] * scale


def attn_bwd(lo, hi, q, k, v, do, o, lse, dqrow, dkcol, BQ=256, BK=256, mode=0):
    R, C = q.shape
    pairs = C // 128
    blk = pl.BlockSpec((R, 128), lambda p, *_: (0, p))
    f32 = jax.ShapeDtypeStruct((R, C), jnp.float32)
    return pl.pallas_call(
        functools.partial(attn_bwd_body, BQ, BK, mode),
        out_shape=(f32, f32, f32),
        grid_spec=pltpu.PrefetchScalarGridSpec(
            num_scalar_prefetch=2, grid=(pairs,),
            in_specs=[blk] * 6 + [pl.BlockSpec((1, R), lambda p, *_: (0, 0)), pl.BlockSpec((R, 1), lambda p, *_: (0, 0))],
            out_specs=[blk, blk, blk],
            scratch_shapes=[pltpu.VMEM((8, 128), jnp.float32)] * 3),
        cost_estimate=pl.CostEstimate(flops=pairs * 2 * R * R * 64 * 10, bytes_accessed=R * C * 24, transcendentals=pairs * 2 * R * R),
        name="attn_bwd",
    )(lo, hi, q, k, v, do, o, lse, dqrow, dkcol)


def ranges(lens, R, BQ, BK):
    ends = jnp.cumsum(lens)
    rid = jnp.arange(R)
    passed = (rid[:, None] >= ends[None, :]).astype(jnp.int32)
    doc = jnp.sum(passed, 1)
    st = jnp.sum(passed * lens[None, :], 1)
    en = jnp.sum(jnp.where(doc[:, None] == jnp.arange(lens.shape[0])[None, :], ends[None, :], 0), 1)
    lo = st[::BQ] // BK
    hi = (en[BQ - 1::BQ] + BK - 1) // BK
    return doc, (rid - st).astype(jnp.float32), lo.astype(jnp.int32), hi.astype(jnp.int32)


F32 = jnp.float32
BF16 = jnp.bfloat16
SWAP = [(0, 1), (1, 0)]


def swap(values, axis):
    return lax.ppermute(values, axis, SWAP)


def rope_tables(positions):
    lane = jnp.arange(128, dtype=jnp.int32)
    frequency = jnp.exp((lane % 32).astype(F32) * (-2.0 * math.log(rope_base) / HEAD_DIM))
    angles = positions[:, None] * frequency[None, :]
    sign = jnp.where(lane % 64 < 32, -1.0, 1.0).astype(F32)
    return jnp.cos(angles), jnp.sin(angles) * sign[None, :]


def rotate(values, cosine, sine):
    rows, width = values.shape
    parts = values.reshape(rows, width // 64, 2, 32)
    turned = jnp.stack([parts[:, :, 1], parts[:, :, 0]], axis=2).reshape(rows, width)
    tiles = width // 128
    return values * jnp.tile(cosine, (1, tiles)) + turned * jnp.tile(sine, (1, tiles))


def layer_norm(summed, gain_row, bias_row):
    centred = summed - jnp.mean(summed, axis=-1, keepdims=True)
    inv_std = lax.rsqrt(jnp.mean(centred * centred, axis=-1, keepdims=True) + norm_eps)
    normed = centred * inv_std
    return (normed * gain_row + bias_row, normed, inv_std)


def norm_back(grad_out, normed, inv_std, gain_row):
    e = grad_out * gain_row
    return inv_std * (
        e - jnp.mean(e, axis=-1, keepdims=True) - normed * jnp.mean(e * normed, axis=-1, keepdims=True)
    )


def dot(a, b, dims):
    return lax.dot_general(a, b, (dims, ((), ())), preferred_element_type=F32)


def both(partial):
    partial = partial.astype(BF16)
    other = swap(partial, "core")
    return partial.astype(F32) + other.astype(F32)


def forward_layer(x, xb, mats, norm_rows, tables, ids):
    wq, wo, wg, wd = mats
    lo, hi, col, row = ids
    width = wo.shape[1]
    projected = dot(xb, wq, ((1,), (0,)))
    q = rotate(projected[:, :width], *tables).astype(BF16)
    k = rotate(projected[:, width : 2 * width], *tables).astype(BF16)
    v = projected[:, 2 * width :].astype(BF16)
    o, lse = attn_fwd(lo, hi, q, k, v, col, row, 512, 512)
    a = both(dot(o, wo, ((1,), (1,))))
    h, n1, r1 = layer_norm(x + a, norm_rows[0], norm_rows[1])
    hb = h.astype(BF16)
    half = wd.shape[1]
    gate_up = dot(hb, wg, ((1,), (0,)))
    m = (jax.nn.silu(gate_up[:, :half]) * gate_up[:, half:]).astype(BF16)
    f = both(dot(m, wd, ((1,), (1,))))
    y, n2, r2 = layer_norm(h + f, norm_rows[2], norm_rows[3])
    return (xb, q, k, v, o, lse, n1, r1, hb, gate_up, m, n2, r2), y


def backward_layer(dy, mats, norm_rows, kept, tables, ids):
    xb, q, k, v, o, lse, n1, r1, hb, gate_up, m, n2, r2 = kept
    wq, wo, wg, wd = mats
    lo, hi, col, row = ids
    half = wd.shape[1]
    gain2 = jnp.sum(dy * n2, axis=0)
    bias2 = jnp.sum(dy, axis=0)
    dz2 = norm_back(dy, n2, r2, norm_rows[2])
    dzb2 = dz2.astype(BF16)
    g_down = dot(dzb2, m, ((0,), (0,)))
    dm = dot(dzb2, wd, ((1,), (0,)))
    gate, up = gate_up[:, :half], gate_up[:, half:]
    sig = jax.nn.sigmoid(gate)
    dub = jnp.concatenate(
        [dm * up * sig * (1.0 + gate * (1.0 - sig)), dm * gate * sig], axis=1
    ).astype(BF16)
    g_gate = dot(hb, dub, ((0,), (0,)))
    dh = both(dot(dub, wg, ((1,), (1,)))) + dz2
    gain1 = jnp.sum(dh * n1, axis=0)
    bias1 = jnp.sum(dh, axis=0)
    dz1 = norm_back(dh, n1, r1, norm_rows[0])
    dzb1 = dz1.astype(BF16)
    g_proj = dot(dzb1, o, ((0,), (0,)))
    do = dot(dzb1, wo, ((1,), (0,))).astype(BF16)
    gq, gk, gv = attn_bwd(lo, hi, q, k, v, do, o, lse, row, col, 512, 512)
    cosine, sine = tables
    dpb = jnp.concatenate([rotate(gq, cosine, -sine), rotate(gk, cosine, -sine), gv], axis=1).astype(BF16)
    g_qkv = dot(xb, dpb, ((0,), (0,)))
    dx = both(dot(dpb, wq, ((1,), (1,)))) + dz1
    return (g_qkv, g_proj, g_gate, g_down), jnp.stack([gain1, bias1, gain2, bias2]), dx


def update(weight, gradient, moment, average, rate):
    moment_new = keep_rate * moment + gradient
    weight_new = weight - rate * (gradient + keep_rate * moment_new)
    average_new = keep_rate * average + (1.0 - keep_rate) * weight_new
    return (gradient, weight_new, moment_new, average_new)


def gather(shard, splits):
    rows, cols = shard.shape
    whole = lax.all_gather(shard, ("dp", "tx"), axis=0, tiled=True)
    return whole.reshape(-1, splits, rows, cols).transpose(1, 0, 2, 3).reshape(splits, -1, cols)


def scatter(parts, rows):
    splits, _, cols = parts.shape
    laid = parts.astype(BF16).reshape(splits, -1, rows, cols).transpose(1, 0, 2, 3).reshape(-1, cols)
    return lax.psum_scatter(laid, ("dp", "tx"), scatter_dimension=0, tiled=True).astype(F32)


def per_device(
    hidden_in, cotangent, lengths, deal, inverse, micro,
    qkv_weight, proj_weight, gate_up_weight, down_weight, norm_params,
    qkv_momentum, proj_momentum, gate_up_momentum, down_momentum, norm_momentum,
    qkv_average, proj_average, gate_up_average, down_average, norm_average,
):
    layers, rows = qkv_weight.shape[:2]
    heads_w = proj_weight.shape[2]
    hid_w = down_weight.shape[2]
    batches = micro.shape[1]
    local_rows, width = hidden_in.shape
    group_rows = deal.shape[0]
    pack_rows = group_rows // batches
    tx = lax.axis_index("tx")
    core = lax.axis_index("core")
    group_base = lax.axis_index("dp") * group_rows

    def four(block):
        pair = jnp.concatenate([block, swap(block, "tx")], axis=0)
        return jnp.concatenate([pair, swap(pair, "core")], axis=0)

    pack = lax.dynamic_index_in_dim(micro[0], tx, 0, keepdims=False)
    wanted = lax.dynamic_slice_in_dim(deal, pack * pack_rows, pack_rows, 0) - group_base
    block = wanted // local_rows
    place = jnp.where(block % 2 != core, 2, 0) + jnp.where(block // 2 != tx, 1, 0)
    source = place * local_rows + wanted % local_rows
    xb = four(hidden_in)[source]

    lens = lax.dynamic_index_in_dim(lengths[0], tx, 0, keepdims=False)
    doc, positions, lo, hi = ranges(lens, pack_rows, 512, 512)
    ids = (lo, hi, doc[:, None], doc[None, :])
    tables = rope_tables(positions)

    mats = []
    for i in range(layers):
        shard_a = jnp.concatenate(
            [qkv_weight[i].reshape(rows, 3 * heads_w), proj_weight[i]], axis=1
        ).astype(BF16)
        shard_b = jnp.concatenate(
            [gate_up_weight[i].reshape(rows, 2 * hid_w), down_weight[i]], axis=1
        ).astype(BF16)
        wa = gather(shard_a, 2)
        wb = gather(shard_b, 2)

        def side(w, first, count, each):
            return jnp.concatenate(
                [w[t][:, (first + c) * each : (first + c + 1) * each] for c in range(count) for t in range(2)], axis=1
            )

        mats.append((
            side(wa, 0, 3, heads_w), side(wa, 3, 1, heads_w), side(wb, 0, 2, hid_w), side(wb, 2, 1, hid_w)
        ))

    x = xb.astype(F32)
    stash = []
    for i in range(layers):
        kept, x = forward_layer(x, xb, mats[i], norm_params[i], tables, ids)
        xb = x.astype(BF16)
        stash.append(kept)

    def arrivals(values):
        half = pack_rows // 2
        mine = lax.dynamic_slice_in_dim(values, core * half, half, 0)
        far = swap(mine, "tx")
        near = swap(far, "core")
        other = jnp.where(core == 0, jnp.concatenate([far, near]), jnp.concatenate([near, far]))
        slots = lax.dynamic_slice_in_dim(inverse, (tx * 2 + core) * local_rows, local_rows, 0) - group_base
        held = slots // pack_rows == pack
        at = jnp.where(held, 0, pack_rows) + slots % pack_rows
        return jnp.concatenate([values, other])[at].astype(F32)

    block_out = arrivals(xb)

    grad = four(cotangent)[source].astype(F32)
    shares = [None] * layers
    norm_sums = [None] * layers
    for i in range(layers - 1, -1, -1):
        (g_qkv, g_proj, g_gate, g_down), norm_sums[i], grad = backward_layer(
            grad, mats[i], norm_params[i], stash[i], tables, ids
        )

        def sides(g, count, each):
            return [
                jnp.concatenate([g[:, (2 * c + t) * each : (2 * c + t + 1) * each] for c in range(count)], axis=1)
                for t in range(2)
            ]

        gu, dn = sides(g_gate, 2, hid_w), sides(g_down, 1, hid_w)
        qk, pr = sides(g_qkv, 3, heads_w), sides(g_proj, 1, heads_w)
        share_b = scatter(jnp.stack([jnp.concatenate([gu[t], dn[t]], axis=1) for t in range(2)]), rows)
        share_a = scatter(jnp.stack([jnp.concatenate([qk[t], pr[t]], axis=1) for t in range(2)]), rows)
        shares[i] = (
            share_a[:, : 3 * heads_w].reshape(rows, 3, heads_w),
            share_a[:, 3 * heads_w :],
            share_b[:, : 2 * hid_w].reshape(rows, 2, hid_w),
            share_b[:, 2 * hid_w :],
        )
    input_grad = arrivals(grad.astype(BF16))
    norm_total = lax.psum(0.5 * jnp.stack(norm_sums), ("dp", "tx", "core"))

    total_tokens = local_rows * lax.axis_size("dp") * lax.axis_size("tx") * lax.axis_size("core")
    proj_fan = max(1, D * 8 // SEQ_MOST)
    grads = [jnp.stack([shares[i][w] for i in range(layers)]) for w in range(4)]
    states = (
        update(qkv_weight, grads[0], qkv_momentum, qkv_average, step_size / math.sqrt(total_tokens * D)),
        update(proj_weight, grads[1], proj_momentum, proj_average, step_size / math.sqrt(total_tokens * proj_fan)),
        update(gate_up_weight, grads[2], gate_up_momentum, gate_up_average, step_size / math.sqrt(total_tokens * D)),
        update(down_weight, grads[3], down_momentum, down_average, step_size / math.sqrt(total_tokens * FF)),
        update(norm_params, norm_total, norm_momentum, norm_average, norm_step / math.sqrt(total_tokens)),
    )
    return (block_out, input_grad) + tuple(v for s in states for v in s)


def solution(mesh):
    dp, tensor = mesh.devices.shape
    fine = Mesh(mesh.devices.reshape(dp, 2, tensor // 2), ("dp", "tx", "core"))
    T = ("tx", "core")
    row = P(("dp",) + T, None)
    w4 = P(None, "dp", None, T)
    w3 = P(None, "dp", T)
    state = (w4, w3, w4, w3, P())
    placed = (row, row, P("dp", None, None), P("dp"), P("dp"), P("dp", None)) + state * 3
    outs = (row, row) + (w4,) * 4 + (w3,) * 4 + (w4,) * 4 + (w3,) * 4 + (P(),) * 4
    return jax.shard_map(per_device, mesh=fine, in_specs=placed, out_specs=outs, check_vma=False)
```

time: 2360 us -> 1190 us (0.50)
  waiting for transfers between devices: 1320 us -> 382 us
  matrix products: 421 us -> 186 us
  blocking collectives: 180 us -> 41.3 us
  Pallas kernels: 0 us -> 122 us
  other arithmetic: 237 us -> 162 us
  starting transfers between devices: 4.29 us -> 63.3 us
  local copies, waits for them, and re-layouts: 169 us -> 214 us
    reduce_scatter x24 -> x4, waiting for transfers between devices: 1020 us -> 258 us  [scatter(): lax.psum_scatter(laid, ('dp', 'tx'), scatter_dimension=0, tiled=True)]
    all_gather x22 -> x4, waiting for transfers between devices: 298 us -> 41.4 us  [gather(): whole = lax.all_gather(shard, ('dp', 'tx'), axis=0, tiled=True)]
    dot_general x116 -> x24, matrix products: 407 us -> 186 us  [dot(): return lax.dot_general(a, b, (dims, ((), ())), preferred_element_type=F32)]
    all_gather x4 -> x0, blocking collectives: 139 us -> none  [the longest x2 77.4 us: per_device(): lax.all_gather(qkv_weight[layer_idx].astype(jnp.bfloat16), 'dp', axis=0,...]
    pallas_call x0 -> x4, Pallas kernels: none -> 122 us  [the longest x2 62.4 us: attn_bwd(): pl.pallas_call(functools.partial(attn_bwd_body, BQ, BK, mode), out_shape=...]
    ppermute x0 -> x16, waiting for transfers between devices: none -> 82.4 us  [swap(): return lax.ppermute(values, axis, SWAP)]
    convert_element_type x31 -> x12, other arithmetic: 104 us -> 41.5 us  [the longest x2 16.7 us: forward_layer(): m = (jax.nn.silu(gate_up[:, :half]) * gate_up[:, half:]).astype(BF16)]
    ppermute x0 -> x16, starting transfers between devices: none -> 62.2 us  [swap(): return lax.ppermute(values, axis, SWAP)]
  transfers between devices with their start and end apart: 46 -> 24, of which waited for: 36 -> 9; matrix products, arithmetic and copies ran while one was open for 28% -> 35% of each run, Pallas kernels for 0% -> 8%
where the time goes in v1:
time: 1190 us
  waiting for transfers between devices  382 us (32%)
  local copies, waits for them, and re-layouts  214 us (18%)
  matrix products  186 us (16%)
  other arithmetic  162 us (14%)
  Pallas kernels  122 us (10%)
  starting transfers between devices  63.3 us (5%)
  blocking collectives  41.3 us (3%)
  between operations  17.2 us (1%)
    reduce_scatter x4, waiting for transfers between devices, scatter(): lax.psum_scatter(laid, ('dp', 'tx'), scatter_dimension=0, tiled=True)  258 us
    dot_general x24, matrix products, dot(): return lax.dot_general(a, b, (dims, ((), ())), preferred_element_type=F32)  186 us
    ppermute x16, waiting for transfers between devices, swap(): return lax.ppermute(values, axis, SWAP)  82.4 us
    pallas_call x2, Pallas kernels, attn_bwd(): pl.pallas_call(functools.partial(attn_bwd_body, BQ, BK, mode), out_shape=...  62.4 us
    ppermute x16, starting transfers between devices, swap(): return lax.ppermute(values, axis, SWAP)  62.2 us
    pallas_call x2, Pallas kernels, attn_fwd(): pl.pallas_call(functools.partial(attn_fwd_body, BQ, BK), out_shape=(jax.S...  59.6 us
    all_gather x4, waiting for transfers between devices, gather(): whole = lax.all_gather(shard, ('dp', 'tx'), axis=0, tiled=True)  41.4 us
    psum x1, blocking collectives, per_device(): norm_total = lax.psum(0.5 * jnp.stack(norm_sums), ('dp', 'tx', 'core'))  41.3 us
  transfers between devices with their start and end apart: 24, of which 9 were waited for; matrix products, arithmetic and copies ran while one was open for 35% of the time, Pallas kernels for 8%

profile of v1, /device:TPU:0, one launch (start us, length us, event | category | flops | bytes accessed | tf_op | source)
XLA Modules:
  0.0 1187.8 jit_solution(3581733734734824930)
XLA Ops:
  18.2 30.5 %collective-permute-done = bf16[768,768]{1,0:T(8,128)(2,1)S(1)} collective-permute-done((bf16[768,768]{1,0:T(8,128)(2,1)S(1)}, bf16[768,768]{1,0:T(8,128)(2,1)S(1)}, u32[]{:S(2)}, u32[]{:S(2)}) %collective-permute-start) | collective-permute-done | bytes 1179680 | tf_op jit(solution)/shard_map/ppermute | solution.py:177
  130.9 30.0 %attn_fwd.2 = (bf16[1536,384]{1,0:T(8,128)(2,1)}, f32[1536,384]{1,0:T(8,128)}) custom-call(s32[3]{0:T(128)} %get-tuple-element.298.lo_ref, s32[3]{0:T(128)} %get-tuple-element.297.hi_ref, bf16[1536,384]{1,0:T(8,128)(2,1)} %get-tuple-element.190.q_ref, bf16[1536,384]{1,0:T(8,128)(2,1)} %get-tuple-element.189.k_ref, bf16[1536,384]{1,0:T(8,128)(2,1)} %slice.705.v_ref, ...), custom_call_target="tpu_custom_call" | custom-call | flops 3623878656 | bytes 7077888 | tf_op jit(solution)/shard_map/attn_fwd/pallas_call | solution.py:77
  188.8 15.1 %fusion.29 = f32[1536,3072]{1,0:T(8,128)} fusion(bf16[768,768]{1,0:T(8,128)(2,1)} %get-tuple-element.308, bf16[768,768]{1,0:T(8,128)(2,1)S(1)} %get-tuple-element.219, bf16[768,768]{1,0:T(8,128)(2,1)} %get-tuple-element.307, bf16[768,768]{1,0:T(8,128)(2,1)S(1)} %get-tuple-element.220, f32[1536,768]{0,1:T(8,128)S(1)} %bitcast.120, f32[768]{0:T(1024)S(1)} %copy-done.86, ...), kind=kOutput, calls=%fused_computation.141 | convolution fusion | flops 7272529920 | bytes 28329984 | tf_op jit(solution)/shard_map/dot_general | solution.py:211
  217.6 15.4 %collective-permute-start.8 = (bf16[768,768]{1,0:T(8,128)(2,1)S(1)}, bf16[768,768]{1,0:T(8,128)(2,1)}, u32[]{:S(2)}, u32[]{:S(2)}) collective-permute-start(bf16[768,768]{1,0:T(8,128)(2,1)S(1)} %copy-done.32), channel_id=1, source_target_pairs={{0,2},{2,0},{1,3},{3,1},{4,6},{6,4},{5,7},{7,5},{8,10},{10,8},{9,1... | collective-permute-start | bytes 3538952 | tf_op jit(solution)/shard_map/ppermute | solution.py:177
  233.0 22.0 %all-gather.9.cloned.1.call-done = bf16[1536,768]{1,0:T(8,128)(2,1)} async-done(((bf16[96,768]{1,0:T(8,128)(2,1)}), bf16[1536,768]{1,0:T(8,128)(2,1)}) %all-gather.9.cloned.1.call-update) | async-done | bytes 2359312 | tf_op jit(solution)/shard_map/all_gather | solution.py:281
  306.0 29.7 %attn_fwd.3 = (bf16[1536,384]{1,0:T(8,128)(2,1)}, f32[1536,384]{1,0:T(8,128)}) custom-call(s32[3]{0:T(128)} %get-tuple-element.298.lo_ref, s32[3]{0:T(128)} %get-tuple-element.297.hi_ref, bf16[1536,384]{1,0:T(8,128)(2,1)} %get-tuple-element.188.q_ref, bf16[1536,384]{1,0:T(8,128)(2,1)} %get-tuple-element.187.k_ref, bf16[1536,384]{1,0:T(8,128)(2,1)} %slice.704.v_ref, ...), custom_call_target="tpu_custom_call" | custom-call | flops 3623878656 | bytes 7077888 | tf_op jit(solution)/shard_map/attn_fwd/pallas_call | solution.py:77
  342.1 15.6 %all-gather.11.cloned.1.call-done = bf16[1536,2304]{1,0:T(8,128)(2,1)} async-done(((bf16[96,2304]{1,0:T(8,128)(2,1)}), bf16[1536,2304]{1,0:T(8,128)(2,1)}) %all-gather.11.cloned.1.call-update) | async-done | bytes 7077904 | tf_op jit(solution)/shard_map/all_gather | solution.py:281
  369.8 13.0 %fusion.28 = f32[1536,3072]{1,0:T(8,128)} fusion(bf16[768,768]{1,0:T(8,128)(2,1)S(1)} %get-tuple-element.311, bf16[768,768]{1,0:T(8,128)(2,1)S(1)} %get-tuple-element.213, bf16[768,768]{1,0:T(8,128)(2,1)S(1)} %get-tuple-element.310, bf16[768,768]{1,0:T(8,128)(2,1)S(1)} %get-tuple-element.214, f32[1536,768]{0,1:T(8,128)S(1)} %get-tuple-element.178, ...), kind=kOutput, calls=%fused_computation.140 | convolution fusion | flops 7272529920 | bytes 28329984 | tf_op jit(solution)/shard_map/dot_general | solution.py:211
  400.1 10.0 gather_fusion.2
  422.3 15.2 %multiply_convert_fusion.3 = (bf16[1536,1536]{1,0:T(8,128)(2,1)}, bf16[1536,1536]{1,0:T(8,128)(2,1)}) fusion(f32[1536,3072]{1,0:T(8,128)} %fusion.28, bf16[768,768]{1,0:T(8,128)(2,1)} %get-tuple-element.312, bf16[768,768]{1,0:T(8,128)(2,1)} %get-tuple-element.212, f32[1536]{0:T(1024)S(1)} %broadcast_multiply_fusion.6, ...), kind=kOutput, calls=%fused_computation.9 | convolution fusion | flops 3669884928 | bytes 37776384 | tf_op jit(solution)/shard_map/dot_general | solution.py:211
  437.5 14.1 %fusion.16 = bf16[1536,768]{0,1:T(8,128)(2,1)} fusion(bf16[1536,1536]{1,0:T(8,128)(2,1)} %get-tuple-element.186, bf16[1536,1536]{1,0:T(8,128)(2,1)} %get-tuple-element.185, bf16[768,768]{1,0:T(8,128)(2,1)} %copy-done.30, bf16[768,768]{1,0:T(8,128)(2,1)} %copy-done.27, bf16[768,768]{1,0:T(8,128)(2,1)} %copy-done.29, bf16[768,768]{1,0:T(8,128)(2,1)} %copy-done.28), kind=kOutput, calls=%fused_computation.79 | convolution fusion | flops 7286685696 | bytes 16515072 | tf_op jit(solution)/shard_map/dot_general | solution.py:211
  456.9 10.2 multiply_reduce_fusion
  471.0 31.3 %attn_bwd.2 = (f32[1536,384]{1,0:T(8,128)}, f32[1536,384]{1,0:T(8,128)}, f32[1536,384]{1,0:T(8,128)}) custom-call(s32[3]{0:T(128)} %get-tuple-element.298.lo_ref, s32[3]{0:T(128)} %get-tuple-element.297.hi_ref, bf16[1536,384]{1,0:T(8,128)(2,1)} %get-tuple-element.188.q_ref, bf16[1536,384]{1,0:T(8,128)(2,1)} %get-tuple-element.187.k_ref, ...), custom_call_target="tpu_custom_call" | custom-call | flops 9059696640 | bytes 14155776 | tf_op jit(solution)/shard_map/attn_bwd/pallas_call | solution.py:146
  533.8 16.5 %multiply_convert_fusion.1 = (bf16[1536,1536]{1,0:T(8,128)(2,1)}, bf16[1536,1536]{1,0:T(8,128)(2,1)}) fusion(f32[1536,3072]{1,0:T(8,128)} %fusion.29, bf16[768,768]{1,0:T(8,128)(2,1)} %get-tuple-element.309, bf16[768,768]{1,0:T(8,128)(2,1)S(1)} %copy-done.57, f32[1536,768]{0,1:T(8,128)S(1)} %subtract_multiply_fusion.1), kind=kOutput, calls=%fused_computation.7 | convolution fusion | flops 3660447744 | bytes 35389440 | tf_op jit(solution)/shard_map/dot_general | solution.py:211
  550.3 14.0 %fusion.17 = bf16[1536,768]{0,1:T(8,128)(2,1)} fusion(bf16[1536,1536]{1,0:T(8,128)(2,1)} %get-tuple-element.184, bf16[1536,1536]{1,0:T(8,128)(2,1)} %get-tuple-element.183, bf16[768,768]{1,0:T(8,128)(2,1)} %get-tuple-element.308, bf16[768,768]{1,0:T(8,128)(2,1)} %copy-done.25, bf16[768,768]{1,0:T(8,128)(2,1)} %get-tuple-element.307, ...), kind=kOutput, calls=%fused_computation.80 | convolution fusion | flops 7286685696 | bytes 16515072 | tf_op jit(solution)/shard_map/dot_general | solution.py:211
  589.6 31.1 %attn_bwd.3 = (f32[1536,384]{1,0:T(8,128)}, f32[1536,384]{1,0:T(8,128)}, f32[1536,384]{1,0:T(8,128)}) custom-call(s32[3]{0:T(128)} %get-tuple-element.298.lo_ref, s32[3]{0:T(128)} %get-tuple-element.297.hi_ref, bf16[1536,384]{1,0:T(8,128)(2,1)} %get-tuple-element.190.q_ref, bf16[1536,384]{1,0:T(8,128)(2,1)} %get-tuple-element.189.k_ref, ...), custom_call_target="tpu_custom_call" | custom-call | flops 9059696640 | bytes 14155776 | tf_op jit(solution)/shard_map/attn_bwd/pallas_call | solution.py:146
  656.5 12.8 %fusion.7 = bf16[768,3072]{1,0:T(8,128)(2,1)S(1)} fusion(bf16[1536,1536]{1,0:T(8,128)(2,1)} %get-tuple-element.186, bf16[1536,1536]{1,0:T(8,128)(2,1)} %get-tuple-element.185, f32[1536,768]{0,1:T(8,128)} %copy-done.2, f32[768]{0:T(1024)S(1)} %copy-done.89, f32[768]{0:T(1024)S(1)} %copy-done.76, f32[1536]{0:T(1024)S(1)} %copy-done.85, f32[1536]{0:T(1024)S(1)} %copy-done.80), kind=kOutput, calls=%fused_computation.26 | convolution fusion | flops 7274889216 | bytes 18892800 | tf_op jit(solution)/shard_map/dot_general | solution.py:211
  684.3 12.7 %fusion.8 = bf16[768,3072]{1,0:T(8,128)(2,1)S(1)} fusion(bf16[1536,1536]{1,0:T(8,128)(2,1)} %get-tuple-element.184, bf16[1536,1536]{1,0:T(8,128)(2,1)} %get-tuple-element.183, f32[1536,768]{0,1:T(8,128)} %copy-done.3, f32[768]{0:T(1024)S(1)} %copy-done.87, f32[768]{0:T(1024)S(1)} %copy-done.74, f32[1536]{0:T(1024)S(1)} %copy-done.82, f32[1536]{0:T(1024)S(1)} %copy-done.78), kind=kOutput, calls=%fused_computation.27 | convolution fusion | flops 7274889216 | bytes 18892800 | tf_op jit(solution)/shard_map/dot_general | solution.py:211
  711.7 39.9 %collective-permute-start.6 = (bf16[768,768]{0,1:T(8,128)(2,1)S(1)}, bf16[768,768]{0,1:T(8,128)(2,1)}, u32[]{:S(2)}, u32[]{:S(2)}) collective-permute-start(bf16[768,768]{0,1:T(8,128)(2,1)S(1)} %constant_dynamic-slice_fusion), channel_id=1, source_target_pairs={{0,2},{2,0},{1,3},{3,1},{4,6},{6,4},{5,7},{7,5},{8,10},{10,8},{9,1... | collective-permute-start | bytes 3538952 | tf_op jit(solution)/shard_map/ppermute | solution.py:177
  751.6 29.0 %collective-permute-done.6 = bf16[768,768]{0,1:T(8,128)(2,1)} collective-permute-done((bf16[768,768]{0,1:T(8,128)(2,1)S(1)}, bf16[768,768]{0,1:T(8,128)(2,1)}, u32[]{:S(2)}, u32[]{:S(2)}) %collective-permute-start.6) | collective-permute-done | bytes 1179680 | tf_op jit(solution)/shard_map/ppermute | solution.py:177
  800.7 18.4 %collective-permute-done.14 = bf16[768,768]{0,1:T(8,128)(2,1)} collective-permute-done((bf16[768,768]{0,1:T(8,128)(2,1)}, bf16[768,768]{0,1:T(8,128)(2,1)}, u32[]{:S(2)}, u32[]{:S(2)}) %collective-permute-start.14) | collective-permute-done | bytes 1179680 | tf_op jit(solution)/shard_map/ppermute | solution.py:177
  838.7 41.3 %psum.7 = f32[2,4,768]{2,1,0:T(4,128)S(1)} all-reduce(f32[2,4,768]{2,1,0:T(4,128)S(1)} %maximum_multiply_fusion), channel_id=1, replica_groups=mesh['dp'=8,'tx'=2,'core'=2] {'dp','tx','core'}, use_global_device_ids=true, to_apply=%region_32.33 | all-reduce | flops 6144 | bytes 49152 | tf_op jit(solution)/shard_map/psum | solution.py:389
  910.9 103.4 %reduce-scatter.11.cloned.1.call-done = bf16[96,2304]{1,0:T(8,128)(2,1)} async-done(((bf16[1536,2304]{1,0:T(8,128)(2,1)}), bf16[96,2304]{1,0:T(8,128)(2,1)}) %reduce-scatter.11.cloned.1.call-update) | async-done | bytes 442384 | tf_op jit(solution)/shard_map/reduce_scatter | solution.py:288
  1016.8 154.5 %reduce-scatter.9.cloned.1.call-done = bf16[96,2304]{1,0:T(8,128)(2,1)} async-done(((bf16[1536,2304]{1,0:T(8,128)(2,1)}), bf16[96,2304]{1,0:T(8,128)(2,1)}) %reduce-scatter.9.cloned.1.call-update) | async-done | bytes 442384 | tf_op jit(solution)/shard_map/reduce_scatter | solution.py:288
  (569 shorter events, 444.8 us)
Async XLA Ops:
  7.2 78.3 %all-gather.5.cloned.1.call-start = ((), (), s32[]{:S(2)}) async-start(), calls=%async_computation.4 | async-start | bytes 2506752 | tf_op jit(solution)/shard_map/all_gather | solution.py:281
  11.9 170.9 %all-gather.7.cloned.1.call-start = ((), (), s32[]{:S(2)}) async-start(), calls=%async_computation.5 | async-start | bytes 7520256 | tf_op jit(solution)/shard_map/all_gather | solution.py:281
  15.1 239.9 %all-gather.9.cloned.1.call-start = ((), (), s32[]{:S(2)}) async-start(), calls=%async_computation.6 | async-start | bytes 2506752 | tf_op jit(solution)/shard_map/all_gather | solution.py:281
  15.2 33.5 %collective-permute-start = (bf16[768,768]{1,0:T(8,128)(2,1)S(1)}, bf16[768,768]{1,0:T(8,128)(2,1)S(1)}, u32[]{:S(2)}, u32[]{:S(2)}) collective-permute-start(bf16[768,768]{1,0:T(8,128)(2,1)S(1)} %copy-done.31), channel_id=1, source_target_pairs={{0,2},{2,0},{1,3},{3,1},{4,6},{6,4},{5,7},{7,5},{8,10},{10,8},{9,1... | collective-permute-start | bytes 3538952 | tf_op jit(solution)/shard_map/ppermute | solution.py:177
  51.3 20.6 %collective-permute-start.1 = (bf16[1536,768]{1,0:T(8,128)(2,1)}, bf16[1536,768]{1,0:T(8,128)(2,1)}, u32[]{:S(2)}, u32[]{:S(2)}) collective-permute-start(bf16[1536,768]{1,0:T(8,128)(2,1)} %pad_maximum_fusion.26), channel_id=1, source_target_pairs={{0,1},{1,0},{2,3},{3,2},{4,5},{5,4},{6,7},{7,6},{8,9},{9,8},{10,11... | collective-permute-start | bytes 7077896 | tf_op jit(solution)/shard_map/ppermute | solution.py:177
  52.3 305.4 %all-gather.11.cloned.1.call-start = ((), (), s32[]{:S(2)}) async-start(), calls=%async_computation.7 | async-start | bytes 7520256 | tf_op jit(solution)/shard_map/all_gather | solution.py:281
  165.2 6.4 collective-permute-start.2
  166.6 670.1 %reduce-scatter.7.cloned.1.call-start = ((), (), s32[]{:S(2)}) async-start(), calls=%async_computation.9 | async-start | bytes 2506752 | tf_op jit(solution)/shard_map/reduce_scatter | solution.py:288
  217.6 45.7 %collective-permute-start.3 = (bf16[1536,768]{0,1:T(8,128)(2,1)}, bf16[1536,768]{0,1:T(8,128)(2,1)}, u32[]{:S(2)}, u32[]{:S(2)}) collective-permute-start(bf16[1536,768]{0,1:T(8,128)(2,1)} %convolution_convert_fusion.7), channel_id=1, source_target_pairs={{0,1},{1,0},{2,3},{3,2},{4,5},{5,4},{6,7},{7,6},{8,9},{9,8},{10,11... | collective-permute-start | bytes 7077896 | tf_op jit(solution)/shard_map/ppermute | solution.py:177
  217.6 121.1 %collective-permute-start.8 = (bf16[768,768]{1,0:T(8,128)(2,1)S(1)}, bf16[768,768]{1,0:T(8,128)(2,1)}, u32[]{:S(2)}, u32[]{:S(2)}) collective-permute-start(bf16[768,768]{1,0:T(8,128)(2,1)S(1)} %copy-done.32), channel_id=1, source_target_pairs={{0,2},{2,0},{1,3},{3,1},{4,6},{6,4},{5,7},{7,5},{8,10},{10,8},{9,1... | collective-permute-start | bytes 3538952 | tf_op jit(solution)/shard_map/ppermute | solution.py:177
  338.6 24.6 %collective-permute-start.4 = (bf16[1536,768]{0,1:T(8,128)(2,1)S(1)}, bf16[1536,768]{0,1:T(8,128)(2,1)}, u32[]{:S(2)}, u32[]{:S(2)}) collective-permute-start(bf16[1536,768]{0,1:T(8,128)(2,1)S(1)} %convolution_convert_fusion.8), channel_id=1, source_target_pairs={{0,1},{1,0},{2,3},{3,2},{4,5},{5,4},{6,7},{7,6},{8,9},{9,8},{10,11... | collective-permute-start | bytes 7077896 | tf_op jit(solution)/shard_map/ppermute | solution.py:177
  341.6 54.6 %collective-permute-start.9 = (bf16[1536,768]{1,0:T(8,128)(2,1)}, bf16[1536,768]{1,0:T(8,128)(2,1)}, u32[]{:S(2)}, u32[]{:S(2)}) collective-permute-start(bf16[1536,768]{1,0:T(8,128)(2,1)} %pad_maximum_fusion.33), channel_id=1, source_target_pairs={{0,1},{1,0},{2,3},{3,2},{4,5},{5,4},{6,7},{7,6},{8,9},{9,8},{10,11... | collective-permute-start | bytes 7077896 | tf_op jit(solution)/shard_map/ppermute | solution.py:177
  396.2 16.8 %collective-permute-start.5 = (bf16[1536,768]{0,1:T(8,128)(2,1)}, bf16[1536,768]{0,1:T(8,128)(2,1)}, u32[]{:S(2)}, u32[]{:S(2)}) collective-permute-start(bf16[1536,768]{0,1:T(8,128)(2,1)} %convolution_convert_fusion.6), channel_id=1, source_target_pairs={{0,1},{1,0},{2,3},{3,2},{4,5},{5,4},{6,7},{7,6},{8,9},{9,8},{10,11... | collective-permute-start | bytes 7077896 | tf_op jit(solution)/shard_map/ppermute | solution.py:177
  451.6 5.3 collective-permute-start.10
  524.0 4.6 collective-permute-start.11
  564.3 11.4 collective-permute-start.12
  575.7 305.8 %reduce-scatter.5.cloned.1.call-start = ((), (), s32[]{:S(2)}) async-start(), calls=%async_computation.8 | async-start | bytes 2506752 | tf_op jit(solution)/shard_map/reduce_scatter | solution.py:288
  646.5 367.7 %reduce-scatter.11.cloned.1.call-start = ((), (), s32[]{:S(2)}) async-start(), calls=%async_computation.11 | async-start | bytes 7520256 | tf_op jit(solution)/shard_map/reduce_scatter | solution.py:288
  675.2 496.1 %reduce-scatter.9.cloned.1.call-start = ((), (), s32[]{:S(2)}) async-start(), calls=%async_computation.10 | async-start | bytes 7520256 | tf_op jit(solution)/shard_map/reduce_scatter | solution.py:288
  711.3 69.4 %collective-permute-start.13 = (bf16[1536,768]{0,1:T(8,128)(2,1)}, bf16[1536,768]{0,1:T(8,128)(2,1)}, u32[]{:S(2)}, u32[]{:S(2)}) collective-permute-start(bf16[1536,768]{0,1:T(8,128)(2,1)} %convolution_convert_fusion.4), channel_id=1, source_target_pairs={{0,1},{1,0},{2,3},{3,2},{4,5},{5,4},{6,7},{7,6},{8,9},{9,8},{10,11... | collective-permute-start | bytes 7077896 | tf_op jit(solution)/shard_map/ppermute | solution.py:177
  711.7 68.9 %collective-permute-start.6 = (bf16[768,768]{0,1:T(8,128)(2,1)S(1)}, bf16[768,768]{0,1:T(8,128)(2,1)}, u32[]{:S(2)}, u32[]{:S(2)}) collective-permute-start(bf16[768,768]{0,1:T(8,128)(2,1)S(1)} %constant_dynamic-slice_fusion), channel_id=1, source_target_pairs={{0,2},{2,0},{1,3},{3,1},{4,6},{6,4},{5,7},{7,5},{8,10},{10,8},{9,1... | collective-permute-start | bytes 3538952 | tf_op jit(solution)/shard_map/ppermute | solution.py:177
  780.6 17.3 %collective-permute-start.7 = (bf16[768,768]{0,1:T(8,128)(2,1)}, bf16[768,768]{0,1:T(8,128)(2,1)}, u32[]{:S(2)}, u32[]{:S(2)}) collective-permute-start(bf16[768,768]{0,1:T(8,128)(2,1)} %collective-permute-done.6), channel_id=1, source_target_pairs={{0,1},{1,0},{2,3},{3,2},{4,5},{5,4},{6,7},{7,6},{8,9},{9,8},{10,11... | collective-permute-start | bytes 3538952 | tf_op jit(solution)/shard_map/ppermute | solution.py:177
  787.8 31.3 %collective-permute-start.14 = (bf16[768,768]{0,1:T(8,128)(2,1)}, bf16[768,768]{0,1:T(8,128)(2,1)}, u32[]{:S(2)}, u32[]{:S(2)}) collective-permute-start(bf16[768,768]{0,1:T(8,128)(2,1)} %constant_dynamic-slice_fusion.1), channel_id=1, source_target_pairs={{0,2},{2,0},{1,3},{3,1},{4,6},{6,4},{5,7},{7,5},{8,10},{10,8},{9,1... | collective-permute-start | bytes 3538952 | tf_op jit(solution)/shard_map/ppermute | solution.py:177
  819.2 70.2 %collective-permute-start.15 = (bf16[768,768]{0,1:T(8,128)(2,1)}, bf16[768,768]{0,1:T(8,128)(2,1)}, u32[]{:S(2)}, u32[]{:S(2)}) collective-permute-start(bf16[768,768]{0,1:T(8,128)(2,1)} %collective-permute-done.14), channel_id=1, source_target_pairs={{0,1},{1,0},{2,3},{3,2},{4,5},{5,4},{6,7},{7,6},{8,9},{9,8},{10,11... | collective-permute-start | bytes 3538952 | tf_op jit(solution)/shard_map/ppermute | solution.py:177
  (146 other events, 2414.2 us)
Sparse Core Ops, SparseCore 0:
  12.0 68.3 all-gather.4
  83.8 98.9 all-gather.6
  186.2 68.7 all-gather.8
  258.2 99.4 all-gather.10
  575.8 148.4 reduce-scatter.6
  729.1 128.3 reduce-scatter.4
  862.8 151.4 reduce-scatter.10
  1019.6 151.6 reduce-scatter.8

commit v2 on v1

--- a/solution.py
+++ b/solution.py
@@ -276,16 +276,37 @@
     return (gradient, weight_new, moment_new, average_new)
 
 
-def gather(shard, splits):
-    rows, cols = shard.shape
-    whole = lax.all_gather(shard, ("dp", "tx"), axis=0, tiled=True)
-    return whole.reshape(-1, splits, rows, cols).transpose(1, 0, 2, 3).reshape(splits, -1, cols)
-
-
-def scatter(parts, rows):
-    splits, _, cols = parts.shape
-    laid = parts.astype(BF16).reshape(splits, -1, rows, cols).transpose(1, 0, 2, 3).reshape(-1, cols)
-    return lax.psum_scatter(laid, ("dp", "tx"), scatter_dimension=0, tiled=True).astype(F32)
+def gather(shard):
+    own = lax.all_gather(shard, ("z", "y"), axis=0, tiled=True)
+    return own, swap(own, "tx")
+
+
+def pick(values, index, axis):
+    return lax.dynamic_index_in_dim(values, index, axis, keepdims=False)
+
+
+def halves(sheet, rows, y):
+    laid = sheet.reshape(-1, 2, rows, sheet.shape[-1])
+    return pick(laid, y, 1), pick(laid, 1 - y, 1)
+
+
+def scatter_x(own, other, rows):
+    y = lax.axis_index("y")
+    got = swap(other.astype(BF16), "tx")
+    keep, send = halves(own.astype(F32) + got.astype(F32), rows, y)
+    got = swap(send.astype(BF16), "y")
+    total = (keep + got.astype(F32)).astype(BF16)
+    return lax.psum_scatter(total.reshape(-1, total.shape[-1]), "z", scatter_dimension=0, tiled=True).astype(F32)
+
+
+def scatter_y(own, other, rows):
+    y = lax.axis_index("y")
+    keep_own, send_own = halves(own.astype(F32), rows, y)
+    keep_other, send_other = halves(other.astype(F32), rows, y)
+    got = swap(jnp.stack([send_own, send_other]).astype(BF16), "y").astype(F32)
+    far = swap((keep_other + got[1]).astype(BF16), "tx").astype(F32)
+    total = (keep_own + got[0] + far).astype(BF16)
+    return lax.psum_scatter(total.reshape(-1, total.shape[-1]), "z", scatter_dimension=0, tiled=True).astype(F32)
 
 
 def per_device(
@@ -303,7 +324,7 @@
     pack_rows = group_rows // batches
     tx = lax.axis_index("tx")
     core = lax.axis_index("core")
-    group_base = lax.axis_index("dp") * group_rows
+    group_base = (lax.axis_index("z") * 2 + lax.axis_index("y")) * group_rows
 
     def four(block):
         pair = jnp.concatenate([block, swap(block, "tx")], axis=0)
@@ -323,14 +344,10 @@
 
     mats = []
     for i in range(layers):
-        shard_a = jnp.concatenate(
-            [qkv_weight[i].reshape(rows, 3 * heads_w), proj_weight[i]], axis=1
-        ).astype(BF16)
-        shard_b = jnp.concatenate(
-            [gate_up_weight[i].reshape(rows, 2 * hid_w), down_weight[i]], axis=1
-        ).astype(BF16)
-        wa = gather(shard_a, 2)
-        wb = gather(shard_b, 2)
+        qkv, proj = qkv_weight[i], proj_weight[i]
+        sheets = gather(jnp.concatenate([qkv.reshape(rows, 3 * heads_w), proj], axis=1).astype(BF16))
+        gates = gather(gate_up_weight[i].reshape(rows, 2 * hid_w).astype(BF16))
+        downs = gather(down_weight[i].astype(BF16))
 
         def side(w, first, count, each):
             return jnp.concatenate(
@@ -338,7 +355,7 @@
             )
 
         mats.append((
-            side(wa, 0, 3, heads_w), side(wa, 3, 1, heads_w), side(wb, 0, 2, hid_w), side(wb, 2, 1, hid_w)
+            side(sheets, 0, 3, heads_w), side(sheets, 3, 1, heads_w), side(gates, 0, 2, hid_w), side(downs, 0, 1, hid_w)
         ))
 
     x = xb.astype(F32)
@@ -377,18 +394,19 @@
 
         gu, dn = sides(g_gate, 2, hid_w), sides(g_down, 1, hid_w)
         qk, pr = sides(g_qkv, 3, heads_w), sides(g_proj, 1, heads_w)
-        share_b = scatter(jnp.stack([jnp.concatenate([gu[t], dn[t]], axis=1) for t in range(2)]), rows)
-        share_a = scatter(jnp.stack([jnp.concatenate([qk[t], pr[t]], axis=1) for t in range(2)]), rows)
+        share_d = scatter_y(dn[0], dn[1], rows)
+        share_g = scatter_x(gu[0], gu[1], rows)
+        share_a = scatter_y(*[jnp.concatenate([qk[t], pr[t]], axis=1) for t in range(2)], rows)
         shares[i] = (
             share_a[:, : 3 * heads_w].reshape(rows, 3, heads_w),
             share_a[:, 3 * heads_w :],
-            share_b[:, : 2 * hid_w].reshape(rows, 2, hid_w),
-            share_b[:, 2 * hid_w :],
+            share_g.reshape(rows, 2, hid_w),
+            share_d,
         )
     input_grad = arrivals(grad.astype(BF16))
-    norm_total = lax.psum(0.5 * jnp.stack(norm_sums), ("dp", "tx", "core"))
-
-    total_tokens = local_rows * lax.axis_size("dp") * lax.axis_size("tx") * lax.axis_size("core")
+    norm_total = lax.psum(0.5 * jnp.stack(norm_sums), ("z", "y", "tx", "core"))
+
+    total_tokens = local_rows * 8 * lax.axis_size("z")
     proj_fan = max(1, D * 8 // SEQ_MOST)
     grads = [jnp.stack([shares[i][w] for i in range(layers)]) for w in range(4)]
     states = (
@@ -403,12 +421,12 @@
 
 def solution(mesh):
     dp, tensor = mesh.devices.shape
-    fine = Mesh(mesh.devices.reshape(dp, 2, tensor // 2), ("dp", "tx", "core"))
-    T = ("tx", "core")
-    row = P(("dp",) + T, None)
-    w4 = P(None, "dp", None, T)
-    w3 = P(None, "dp", T)
+    fine = Mesh(mesh.devices.reshape(dp // 2, 2, 2, tensor // 2), ("z", "y", "tx", "core"))
+    G, T = ("z", "y"), ("tx", "core")
+    row = P(G + T, None)
+    w4 = P(None, G, None, T)
+    w3 = P(None, G, T)
     state = (w4, w3, w4, w3, P())
-    placed = (row, row, P("dp", None, None), P("dp"), P("dp"), P("dp", None)) + state * 3
+    placed = (row, row, P(G, None, None), P(G), P(G), P(G, None)) + state * 3
     outs = (row, row) + (w4,) * 4 + (w3,) * 4 + (w4,) * 4 + (w3,) * 4 + (P(),) * 4
     return jax.shard_map(per_device, mesh=fine, in_specs=placed, out_specs=outs, check_vma=False)

time: 1190 us -> 1140 us (0.958)
  waiting for transfers between devices: 382 us -> 242 us
  blocking collectives: 41.3 us -> 110 us
  starting transfers between devices: 63.3 us -> 21.2 us
  other arithmetic: 162 us -> 196 us
  local copies, waits for them, and re-layouts: 214 us -> 233 us
    reduce_scatter x4 -> x6, waiting for transfers between devices: 258 us -> 0.03 us  [the longest x4 0.03 us: scatter_y(): lax.psum_scatter(total.reshape(-1, total.shape[-1]), 'z', scatter_dimensi...]
    ppermute x16 -> x34, waiting for transfers between devices: 82.4 us -> 236 us  [swap(): return lax.ppermute(values, axis, SWAP)]
    psum x1, blocking collectives: 41.3 us -> 110 us  [per_device(): norm_total = lax.psum(0.5 * jnp.stack(norm_sums), ('z', 'y', 'tx', 'core'))]
    ppermute x16 -> x34, starting transfers between devices: 62.2 us -> 20.3 us  [swap(): return lax.ppermute(values, axis, SWAP)]
    all_gather x4 -> x6, waiting for transfers between devices: 41.4 us -> 5.03 us  [gather(): own = lax.all_gather(shard, ('z', 'y'), axis=0, tiled=True)]
    convert_element_type x4 -> x16, other arithmetic: 3.1 us -> 21 us  [the longest x2 6.82 us: scatter_x(): total = (keep + got.astype(F32)).astype(BF16)]
    unnamed x303 -> x328, local copies, waits for them, and re-layouts: 31.2 us -> 37.8 us
  transfers between devices with their start and end apart: 24 -> 46, of which waited for: 9 -> 16; matrix products, arithmetic and copies ran while one was open for 35% -> 47% of each run, Pallas kernels for 8% -> 11%
where the time goes in v2:
time: 1140 us; the launch traced here: 1130 us
  waiting for transfers between devices  242 us (21%)
  local copies, waits for them, and re-layouts  233 us (20%)
  other arithmetic  196 us (17%)
  matrix products  193 us (17%)
  Pallas kernels  122 us (11%)
  blocking collectives  110 us (10%)
  starting transfers between devices  21.2 us (2%)
  between operations  17.4 us (2%)
    ppermute x34, waiting for transfers between devices, swap(): return lax.ppermute(values, axis, SWAP)  236 us
    dot_general x24, matrix products, dot(): return lax.dot_general(a, b, (dims, ((), ())), preferred_element_type=F32)  193 us
    psum x1, blocking collectives, per_device(): norm_total = lax.psum(0.5 * jnp.stack(norm_sums), ('z', 'y', 'tx', 'core'))  110 us
    pallas_call x2, Pallas kernels, attn_bwd(): pl.pallas_call(functools.partial(attn_bwd_body, BQ, BK, mode), out_shape=...  62.4 us
    pallas_call x2, Pallas kernels, attn_fwd(): pl.pallas_call(functools.partial(attn_fwd_body, BQ, BK), out_shape=(jax.S...  59.6 us
    unnamed x328, local copies, waits for them, and re-layouts  37.8 us
    reshape x8, local copies, waits for them, and re-layouts, rotate(): jnp.stack([parts[:, :, 1], parts[:, :, 0]], axis=2).reshape(rows, width)  23.8 us
  transfers between devices with their start and end apart: 46, of which 16 were waited for; matrix products, arithmetic and copies ran while one was open for 47% of the time, Pallas kernels for 11%

profile of v2, /device:TPU:0, one launch (start us, length us, event | category | flops | bytes accessed | tf_op | source)
XLA Modules:
  0.0 1134.5 jit_solution(12353980882459132422)
XLA Ops:
  18.2 26.0 %collective-permute-done = bf16[768,768]{1,0:T(8,128)(2,1)S(1)} collective-permute-done((bf16[768,768]{1,0:T(8,128)(2,1)S(1)}, bf16[768,768]{1,0:T(8,128)(2,1)S(1)}, u32[]{:S(2)}, u32[]{:S(2)}) %collective-permute-start) | collective-permute-done | bytes 1179680 | tf_op jit(solution)/shard_map/ppermute | solution.py:177
  140.5 29.8 %attn_fwd.2 = (bf16[1536,384]{1,0:T(8,128)(2,1)}, f32[1536,384]{1,0:T(8,128)}) custom-call(s32[3]{0:T(128)} %get-tuple-element.291.lo_ref, s32[3]{0:T(128)} %get-tuple-element.290.hi_ref, bf16[1536,384]{1,0:T(8,128)(2,1)} %get-tuple-element.191.q_ref, bf16[1536,384]{1,0:T(8,128)(2,1)} %get-tuple-element.190.k_ref, bf16[1536,384]{1,0:T(8,128)(2,1)} %slice.657.v_ref, ...), custom_call_target="tpu_custom_call" | custom-call | flops 3623878656 | bytes 7077888 | tf_op jit(solution)/shard_map/attn_fwd/pallas_call | solution.py:77
  189.2 39.7 %collective-permute-done.4 = bf16[768,1536]{1,0:T(8,128)(2,1)} collective-permute-done((bf16[768,1536]{1,0:T(8,128)(2,1)}, bf16[768,1536]{1,0:T(8,128)(2,1)}, u32[]{:S(2)}, u32[]{:S(2)}) %collective-permute-start.4) | collective-permute-done | bytes 2359328 | tf_op jit(solution)/shard_map/ppermute | solution.py:177
  230.8 13.0 %fusion.57 = f32[1536,3072]{1,0:T(8,128)} fusion(bf16[768,768]{1,0:T(8,128)(2,1)S(1)} %get-tuple-element.244, bf16[768,768]{1,0:T(8,128)(2,1)S(1)} %get-tuple-element.242, bf16[768,768]{1,0:T(8,128)(2,1)S(1)} %get-tuple-element.243, bf16[768,768]{1,0:T(8,128)(2,1)S(1)} %get-tuple-element.241, f32[1536,768]{0,1:T(8,128)S(1)} %get-tuple-element.183, ...), kind=kOutput, calls=%fused_computation.183 | convolution fusion | flops 7272529920 | bytes 28329984 | tf_op jit(solution)/shard_map/dot_general | solution.py:211
  264.6 24.1 %collective-permute-done.7 = bf16[768,768]{1,0:T(8,128)(2,1)S(1)} collective-permute-done((bf16[768,768]{1,0:T(8,128)(2,1)}, bf16[768,768]{1,0:T(8,128)(2,1)S(1)}, u32[]{:S(2)}, u32[]{:S(2)}) %collective-permute-start.7) | collective-permute-done | bytes 1179680 | tf_op jit(solution)/shard_map/ppermute | solution.py:177
  339.1 29.8 %attn_fwd.3 = (bf16[1536,384]{1,0:T(8,128)(2,1)}, f32[1536,384]{1,0:T(8,128)}) custom-call(s32[3]{0:T(128)} %get-tuple-element.291.lo_ref, s32[3]{0:T(128)} %get-tuple-element.290.hi_ref, bf16[1536,384]{1,0:T(8,128)(2,1)} %get-tuple-element.189.q_ref, bf16[1536,384]{1,0:T(8,128)(2,1)} %get-tuple-element.188.k_ref, bf16[1536,384]{1,0:T(8,128)(2,1)} %slice.656.v_ref, ...), custom_call_target="tpu_custom_call" | custom-call | flops 3623878656 | bytes 7077888 | tf_op jit(solution)/shard_map/attn_fwd/pallas_call | solution.py:77
  373.8 27.8 %collective-permute-done.14 = bf16[768,768]{1,0:T(8,128)(2,1)S(1)} collective-permute-done((bf16[768,768]{1,0:T(8,128)(2,1)S(1)}, bf16[768,768]{1,0:T(8,128)(2,1)S(1)}, u32[]{:S(2)}, u32[]{:S(2)}) %collective-permute-start.14) | collective-permute-done | bytes 1179680 | tf_op jit(solution)/shard_map/ppermute | solution.py:177
  414.6 13.0 %fusion.56 = f32[1536,3072]{1,0:T(8,128)} fusion(bf16[768,768]{1,0:T(8,128)(2,1)S(1)} %get-tuple-element.248, bf16[768,768]{1,0:T(8,128)(2,1)S(1)} %get-tuple-element.246, bf16[768,768]{1,0:T(8,128)(2,1)S(1)} %get-tuple-element.247, bf16[768,768]{1,0:T(8,128)(2,1)S(1)} %get-tuple-element.245, f32[1536,768]{0,1:T(8,128)S(1)} %get-tuple-element.179, ...), kind=kOutput, calls=%fused_computation.182 | convolution fusion | flops 7272529920 | bytes 28329984 | tf_op jit(solution)/shard_map/dot_general | solution.py:211
  446.4 9.8 gather_fusion.2
  468.6 15.2 %multiply_convert_fusion.3 = (bf16[1536,1536]{1,0:T(8,128)(2,1)}, bf16[1536,1536]{1,0:T(8,128)(2,1)}) fusion(f32[1536,3072]{1,0:T(8,128)} %fusion.56, bf16[768,768]{1,0:T(8,128)(2,1)} %collective-permute-done.10, bf16[768,768]{1,0:T(8,128)(2,1)} %bitcast.284, f32[1536]{0:T(1024)S(1)} %broadcast_multiply_fusion.6, f32[1536,768]{0,1:T(8,128)S(1)} %get-tuple-element.177, ...), kind=kOutput, calls=%fused_computation.9 | convolution fusion | flops 3669884928 | bytes 37776384 | tf_op jit(solution)/shard_map/dot_general | solution.py:211
  483.8 13.6 %fusion.14 = bf16[1536,768]{0,1:T(8,128)(2,1)} fusion(bf16[1536,1536]{1,0:T(8,128)(2,1)} %get-tuple-element.187, bf16[1536,1536]{1,0:T(8,128)(2,1)} %get-tuple-element.186, bf16[768,768]{1,0:T(8,128)(2,1)} %copy-done.46, bf16[768,768]{1,0:T(8,128)(2,1)} %copy-done.44, bf16[768,768]{1,0:T(8,128)(2,1)} %copy-done.45, bf16[768,768]{1,0:T(8,128)(2,1)S(1)} %get-tuple-element.245), kind=kOutput, calls=%fused_computation.73 | convolution fusion | flops 7286685696 | bytes 16515072 | tf_op jit(solution)/shard_map/dot_general | solution.py:211
  502.2 18.6 %fusion.144 = (bf16[768,3072]{1,0:T(8,128)(2,1)}, f32[768,3072]{1,0:T(8,128)}) fusion(bf16[1536,1536]{1,0:T(8,128)(2,1)} %get-tuple-element.187, bf16[1536,1536]{1,0:T(8,128)(2,1)} %get-tuple-element.186, f32[1536,768]{0,1:T(8,128)} %copy-done.2, f32[768]{0:T(1024)S(1)} %copy-done.94, f32[768]{0:T(1024)S(1)} %get-tuple-element.148, ...), kind=kOutput, calls=%fused_computation.353 | convolution fusion | flops 7274889216 | bytes 28329984 | tf_op jit(solution)/shard_map/dot_general | solution.py:211
  540.6 31.3 %attn_bwd.2 = (f32[1536,384]{1,0:T(8,128)}, f32[1536,384]{1,0:T(8,128)}, f32[1536,384]{1,0:T(8,128)}) custom-call(s32[3]{0:T(128)} %get-tuple-element.291.lo_ref, s32[3]{0:T(128)} %get-tuple-element.290.hi_ref, bf16[1536,384]{1,0:T(8,128)(2,1)} %get-tuple-element.189.q_ref, bf16[1536,384]{1,0:T(8,128)(2,1)} %get-tuple-element.188.k_ref, ...), custom_call_target="tpu_custom_call" | custom-call | flops 9059696640 | bytes 14155776 | tf_op jit(solution)/shard_map/attn_bwd/pallas_call | solution.py:146
  614.5 21.6 %collective-permute-done.24 = bf16[2,4,96,768]{3,2,1,0:T(8,128)(2,1)} collective-permute-done((bf16[2,4,96,768]{3,2,1,0:T(8,128)(2,1)}, bf16[2,4,96,768]{3,2,1,0:T(8,128)(2,1)}, u32[]{:S(2)}, u32[]{:S(2)}) %collective-permute-start.24) | collective-permute-done | bytes 1179680 | tf_op jit(solution)/shard_map/ppermute | solution.py:177
  660.4 10.2 collective-permute-done.29
  677.5 24.2 %collective-permute-done.32 = bf16[2,4,96,768]{3,2,1,0:T(8,128)(2,1)S(1)} collective-permute-done((bf16[2,4,96,768]{3,2,1,0:T(8,128)(2,1)}, bf16[2,4,96,768]{3,2,1,0:T(8,128)(2,1)S(1)}, u32[]{:S(2)}, u32[]{:S(2)}) %collective-permute-start.32) | collective-permute-done | bytes 1179680 | tf_op jit(solution)/shard_map/ppermute | solution.py:177
  702.2 14.1 %collective-permute-done.33 = bf16[4,96,768]{2,1,0:T(8,128)(2,1)S(1)} collective-permute-done((bf16[4,96,768]{2,1,0:T(8,128)(2,1)S(1)}, bf16[4,96,768]{2,1,0:T(8,128)(2,1)S(1)}, u32[]{:S(2)}, u32[]{:S(2)}) %collective-permute-start.33) | collective-permute-done | bytes 589856 | tf_op jit(solution)/shard_map/ppermute | solution.py:177
  737.8 15.3 %multiply_convert_fusion.1 = (bf16[1536,1536]{1,0:T(8,128)(2,1)}, bf16[1536,1536]{1,0:T(8,128)(2,1)}) fusion(f32[1536,3072]{1,0:T(8,128)} %fusion.57, bf16[768,768]{1,0:T(8,128)(2,1)} %collective-permute-done.5, bf16[768,768]{1,0:T(8,128)(2,1)S(1)} %bitcast.282, f32[1536,768]{0,1:T(8,128)S(1)} %subtract_multiply_fusion.1), kind=kOutput, calls=%fused_computation.7 | convolution fusion | flops 3660447744 | bytes 35389440 | tf_op jit(solution)/shard_map/dot_general | solution.py:211
  753.2 14.0 %fusion.15 = bf16[1536,768]{0,1:T(8,128)(2,1)} fusion(bf16[1536,1536]{1,0:T(8,128)(2,1)} %get-tuple-element.185, bf16[1536,1536]{1,0:T(8,128)(2,1)} %get-tuple-element.184, bf16[768,768]{1,0:T(8,128)(2,1)} %copy-done.43, bf16[768,768]{1,0:T(8,128)(2,1)} %copy-done.41, bf16[768,768]{1,0:T(8,128)(2,1)} %copy-done.42, bf16[768,768]{1,0:T(8,128)(2,1)} %copy-done.40), kind=kOutput, calls=%fused_computation.74 | convolution fusion | flops 7286685696 | bytes 16515072 | tf_op jit(solution)/shard_map/dot_general | solution.py:211
  773.0 16.8 %fusion.145 = (bf16[768,3072]{1,0:T(8,128)(2,1)}, f32[768,3072]{1,0:T(8,128)}) fusion(bf16[1536,1536]{1,0:T(8,128)(2,1)} %get-tuple-element.185, bf16[1536,1536]{1,0:T(8,128)(2,1)} %get-tuple-element.184, f32[1536,768]{0,1:T(8,128)S(1)} %bitcast.208, f32[768]{0:T(1024)S(1)} %copy-done.93, f32[768]{0:T(1024)S(1)} %copy-done.83, f32[1536]{0:T(1024)S(1)} %copy-done.88, ...), kind=kOutput, calls=%fused_computation.354 | convolution fusion | flops 7274889216 | bytes 28329984 | tf_op jit(solution)/shard_map/dot_general | solution.py:211
  813.4 31.1 %attn_bwd.3 = (f32[1536,384]{1,0:T(8,128)}, f32[1536,384]{1,0:T(8,128)}, f32[1536,384]{1,0:T(8,128)}) custom-call(s32[3]{0:T(128)} %get-tuple-element.291.lo_ref, s32[3]{0:T(128)} %get-tuple-element.290.hi_ref, bf16[1536,384]{1,0:T(8,128)(2,1)} %get-tuple-element.191.q_ref, bf16[1536,384]{1,0:T(8,128)(2,1)} %get-tuple-element.190.k_ref, ...), custom_call_target="tpu_custom_call" | custom-call | flops 9059696640 | bytes 14155776 | tf_op jit(solution)/shard_map/attn_bwd/pallas_call | solution.py:146
  888.0 12.9 %collective-permute-done.22 = bf16[2,4,96,768]{3,2,1,0:T(8,128)(2,1)} collective-permute-done((bf16[2,4,96,768]{3,2,1,0:T(8,128)(2,1)}, bf16[2,4,96,768]{3,2,1,0:T(8,128)(2,1)}, u32[]{:S(2)}, u32[]{:S(2)}) %collective-permute-start.22) | collective-permute-done | bytes 1179680 | tf_op jit(solution)/shard_map/ppermute | solution.py:177
  927.2 9.7 collective-permute-done.27
  971.2 110.2 %psum.7 = f32[2,4,768]{2,1,0:T(4,128)S(1)} all-reduce(f32[2,4,768]{2,1,0:T(4,128)S(1)} %maximum_multiply_fusion), channel_id=1, replica_groups=mesh['z'=4,'y'=2,'tx'=2,'core'=2] {'z','y','tx','core'}, use_global_device_ids=true, to_apply=%region_34.35 | all-reduce | flops 6144 | bytes 49152 | tf_op jit(solution)/shard_map/psum | solution.py:407
  (661 shorter events, 545.2 us)
Async XLA Ops:
  7.2 48.6 %all-gather.9.cloned.1.call-start = ((), (), s32[]{:S(2)}) async-start(), calls=%async_computation.6 | async-start | bytes 1327104 | tf_op jit(solution)/shard_map/all_gather | solution.py:280
  11.9 162.6 %all-gather.11.cloned.1.call-start = ((), (), s32[]{:S(2)}) async-start(), calls=%async_computation.7 | async-start | bytes 2654208 | tf_op jit(solution)/shard_map/all_gather | solution.py:280
  14.2 163.2 %all-gather.17.cloned.1.call-start = ((), (), s32[]{:S(2)}) async-start(), calls=%async_computation.16 | async-start | bytes 1327104 | tf_op jit(solution)/shard_map/all_gather | solution.py:280
  15.1 245.0 %all-gather.13.cloned.1.call-start = ((), (), s32[]{:S(2)}) async-start(), calls=%async_computation.8 | async-start | bytes 1327104 | tf_op jit(solution)/shard_map/all_gather | solution.py:280
  46.0 43.7 %collective-permute-start.1 = (bf16[1536,768]{1,0:T(8,128)(2,1)}, bf16[1536,768]{1,0:T(8,128)(2,1)}, u32[]{:S(2)}, u32[]{:S(2)}) collective-permute-start(bf16[1536,768]{1,0:T(8,128)(2,1)} %pad_maximum_fusion.18), channel_id=1, source_target_pairs={{0,1},{1,0},{2,3},{3,2},{4,5},{5,4},{6,7},{7,6},{8,9},{9,8},{10,11... | collective-permute-start | bytes 7077896 | tf_op jit(solution)/shard_map/ppermute | solution.py:177
  47.0 247.7 %all-gather.15.cloned.1.call-start = ((), (), s32[]{:S(2)}) async-start(), calls=%async_computation.9 | async-start | bytes 2654208 | tf_op jit(solution)/shard_map/all_gather | solution.py:280
  174.5 54.4 %collective-permute-start.4 = (bf16[768,1536]{1,0:T(8,128)(2,1)}, bf16[768,1536]{1,0:T(8,128)(2,1)}, u32[]{:S(2)}, u32[]{:S(2)}) collective-permute-start(bf16[768,1536]{1,0:T(8,128)(2,1)} %all-gather.11.cloned.1.call-done), channel_id=1, source_target_pairs={{0,2},{2,0},{1,3},{3,1},{4,6},{6,4},{5,7},{7,5},{8,10},{10,8},{9,1... | collective-permute-start | bytes 7077896 | tf_op jit(solution)/shard_map/ppermute | solution.py:177
  176.7 226.5 %all-gather.19.cloned.1.call-start = ((), (), s32[]{:S(2)}) async-start(), calls=%async_computation.17 | async-start | bytes 1327104 | tf_op jit(solution)/shard_map/all_gather | solution.py:280
  177.5 76.3 %collective-permute-start.5 = (bf16[768,768]{1,0:T(8,128)(2,1)}, bf16[768,768]{1,0:T(8,128)(2,1)}, u32[]{:S(2)}, u32[]{:S(2)}) collective-permute-start(bf16[768,768]{1,0:T(8,128)(2,1)} %bitcast.280), channel_id=1, source_target_pairs={{0,2},{2,0},{1,3},{3,1},{4,6},{6,4},{5,7},{7,5},{8,10},{10,8},{9,1... | collective-permute-start | bytes 3538952 | tf_op jit(solution)/shard_map/ppermute | solution.py:177
  261.7 702.7 %reduce-scatter.9.cloned.1.call-start = ((), (), s32[]{:S(2)}) async-start(), calls=%async_computation.11 | async-start | bytes 737280 | tf_op jit(solution)/shard_map/reduce_scatter | solution.py:309
  294.7 111.3 %collective-permute-start.9 = (bf16[768,1536]{1,0:T(8,128)(2,1)}, bf16[768,1536]{1,0:T(8,128)(2,1)}, u32[]{:S(2)}, u32[]{:S(2)}) collective-permute-start(bf16[768,1536]{1,0:T(8,128)(2,1)} %all-gather.15.cloned.1.call-done), channel_id=1, source_target_pairs={{0,2},{2,0},{1,3},{3,1},{4,6},{6,4},{5,7},{7,5},{8,10},{10,8},{9,1... | collective-permute-start | bytes 7077896 | tf_op jit(solution)/shard_map/ppermute | solution.py:177
  524.4 115.0 %collective-permute-start.28 = (bf16[768,1536]{1,0:T(8,128)(2,1)}, bf16[768,1536]{1,0:T(8,128)(2,1)}, u32[]{:S(2)}, u32[]{:S(2)}) collective-permute-start(bf16[768,1536]{1,0:T(8,128)(2,1)} %pad_maximum_fusion.35), channel_id=1, source_target_pairs={{0,2},{2,0},{1,3},{3,1},{4,6},{6,4},{5,7},{7,5},{8,10},{10,8},{9,1... | collective-permute-start | bytes 7077896 | tf_op jit(solution)/shard_map/ppermute | solution.py:177
  653.5 314.5 %reduce-scatter.13.cloned.1.call-start = ((), (), s32[]{:S(2)}) async-start(), calls=%async_computation.13 | async-start | bytes 1474560 | tf_op jit(solution)/shard_map/reduce_scatter | solution.py:299
  660.3 57.2 %collective-permute-start.17 = (bf16[1536,768]{0,1:T(8,128)(2,1)}, bf16[1536,768]{0,1:T(8,128)(2,1)}, u32[]{:S(2)}, u32[]{:S(2)}) collective-permute-start(bf16[1536,768]{0,1:T(8,128)(2,1)} %convolution_convert_fusion.1), channel_id=1, source_target_pairs={{0,1},{1,0},{2,3},{3,2},{4,5},{5,4},{6,7},{7,6},{8,9},{9,8},{10,11... | collective-permute-start | bytes 7077896 | tf_op jit(solution)/shard_map/ppermute | solution.py:177
  674.0 408.1 %reduce-scatter.17.cloned.1.call-start = ((), (), s32[]{:S(2)}) async-start(), calls=%async_computation.15 | async-start | bytes 737280 | tf_op jit(solution)/shard_map/reduce_scatter | solution.py:309
  677.2 40.3 %collective-permute-start.12 = (bf16[768,768]{0,1:T(8,128)(2,1)}, bf16[768,768]{0,1:T(8,128)(2,1)}, u32[]{:S(2)}, u32[]{:S(2)}) collective-permute-start(bf16[768,768]{0,1:T(8,128)(2,1)} %constant_dynamic-slice_fusion.1), channel_id=1, source_target_pairs={{0,2},{2,0},{1,3},{3,1},{4,6},{6,4},{5,7},{7,5},{8,10},{10,8},{9,1... | collective-permute-start | bytes 3538952 | tf_op jit(solution)/shard_map/ppermute | solution.py:177
  717.4 364.7 %reduce-scatter.15.cloned.1.call-start = ((), (), s32[]{:S(2)}) async-start(), calls=%async_computation.14 | async-start | bytes 737280 | tf_op jit(solution)/shard_map/reduce_scatter | solution.py:309
  717.5 205.4 %collective-permute-start.13 = (bf16[768,768]{0,1:T(8,128)(2,1)}, bf16[768,768]{0,1:T(8,128)(2,1)}, u32[]{:S(2)}, u32[]{:S(2)}) collective-permute-start(bf16[768,768]{0,1:T(8,128)(2,1)} %collective-permute-done.12), channel_id=1, source_target_pairs={{0,1},{1,0},{2,3},{3,2},{4,5},{5,4},{6,7},{7,6},{8,9},{9,8},{10,11... | collective-permute-start | bytes 3538952 | tf_op jit(solution)/shard_map/ppermute | solution.py:177
  793.4 110.2 %collective-permute-start.26 = (bf16[768,1536]{1,0:T(8,128)(2,1)}, bf16[768,1536]{1,0:T(8,128)(2,1)}, u32[]{:S(2)}, u32[]{:S(2)}) collective-permute-start(bf16[768,1536]{1,0:T(8,128)(2,1)} %pad_maximum_fusion.34), channel_id=1, source_target_pairs={{0,2},{2,0},{1,3},{3,1},{4,6},{6,4},{5,7},{7,5},{8,10},{10,8},{9,1... | collective-permute-start | bytes 7077896 | tf_op jit(solution)/shard_map/ppermute | solution.py:177
  801.4 76.8 %collective-permute-start.31 = (bf16[4,96,768]{2,1,0:T(8,128)(2,1)}, bf16[4,96,768]{2,1,0:T(8,128)(2,1)}, u32[]{:S(2)}, u32[]{:S(2)}) collective-permute-start(bf16[4,96,768]{2,1,0:T(8,128)(2,1)} %fusion.30), channel_id=1, source_target_pairs={{0,2},{2,0},{1,3},{3,1},{4,6},{6,4},{5,7},{7,5},{8,10},{10,8},{9,1... | collective-permute-start | bytes 1769480 | tf_op jit(solution)/shard_map/ppermute | solution.py:177
  881.5 203.5 %reduce-scatter.7.cloned.1.call-start = ((), (), s32[]{:S(2)}) async-start(), calls=%async_computation.10 | async-start | bytes 737280 | tf_op jit(solution)/shard_map/reduce_scatter | solution.py:309
  888.0 52.3 %collective-permute-start.19 = (bf16[1536,768]{0,1:T(8,128)(2,1)}, bf16[1536,768]{0,1:T(8,128)(2,1)}, u32[]{:S(2)}, u32[]{:S(2)}) collective-permute-start(bf16[1536,768]{0,1:T(8,128)(2,1)} %convolution_convert_fusion), channel_id=1, source_target_pairs={{0,1},{1,0},{2,3},{3,2},{4,5},{5,4},{6,7},{7,6},{8,9},{9,8},{10,11... | collective-permute-start | bytes 7077896 | tf_op jit(solution)/shard_map/ppermute | solution.py:177
  920.1 180.2 %reduce-scatter.11.cloned.1.call-start = ((), (), s32[]{:S(2)}) async-start(), calls=%async_computation.12 | async-start | bytes 1474560 | tf_op jit(solution)/shard_map/reduce_scatter | solution.py:299
  946.2 140.6 %collective-permute-start.20 = (bf16[768,768]{0,1:T(8,128)(2,1)}, bf16[768,768]{0,1:T(8,128)(2,1)}, u32[]{:S(2)}, u32[]{:S(2)}) collective-permute-start(bf16[768,768]{0,1:T(8,128)(2,1)} %constant_dynamic-slice_fusion), channel_id=1, source_target_pairs={{0,2},{2,0},{1,3},{3,1},{4,6},{6,4},{5,7},{7,5},{8,10},{10,8},{9,1... | collective-permute-start | bytes 3538952 | tf_op jit(solution)/shard_map/ppermute | solution.py:177
  (181 other events, 3154.9 us)
Sparse Core Ops, SparseCore 0:
  12.0 43.7 all-gather.8
  58.5 50.5 all-gather.10
  111.8 39.6 all-gather.16
  154.1 39.7 all-gather.12
  196.0 50.4 all-gather.14
  261.8 55.4 all-gather.18
  653.6 73.5 reduce-scatter.8
  729.5 27.6 reduce-scatter.12
  760.0 30.2 reduce-scatter.16
  881.6 91.2 reduce-scatter.14
  975.8 35.4 reduce-scatter.6
  1014.0 27.6 reduce-scatter.10

commit v3 on v2

--- a/solution.py
+++ b/solution.py
@@ -28,8 +28,25 @@
     return lax.dot_general(a, b, dims, preferred_element_type=jnp.float32)
 
 
-def attn_fwd_body(BQ, BK, lo_ref, hi_ref, q_ref, k_ref, v_ref, dq_ref, dk_ref, o_ref, lse_ref):
+def turn(values, cosine, sine):
+    lane = lax.broadcasted_iota(jnp.int32, values.shape, 1)
+    turned = jnp.where(lane % HEAD_DIM < 32, pltpu.roll(values, 96, 1), pltpu.roll(values, 32, 1))
+    return values * cosine + turned * sine
+
+
+def attn_fwd_body(BQ, BK, lo_ref, hi_ref, pq_ref, pk_ref, pv_ref, cos_ref, sin_ref, dq_ref, dk_ref,
+                  q_ref, k_ref, v_ref, o_ref, lse_ref):
     R = q_ref.shape[0]
+
+    def rope_block(i, _):
+        rows = pl.ds(pl.multiple_of(i * 256, 256), 256)
+        cosine, sine = cos_ref[rows, :], sin_ref[rows, :]
+        q_ref[rows, :] = turn(pq_ref[rows, :], cosine, sine).astype(jnp.bfloat16)
+        k_ref[rows, :] = turn(pk_ref[rows, :], cosine, sine).astype(jnp.bfloat16)
+        v_ref[rows, :] = pv_ref[rows, :].astype(jnp.bfloat16)
+        return 0
+
+    lax.fori_loop(0, R // 256, rope_block, 0)
     lane = lax.broadcasted_iota(jnp.int32, (BQ, 128), 1)
     first = lane < HEAD_DIM
     zero = jnp.zeros((BQ, 128), jnp.bfloat16)
@@ -70,24 +87,28 @@
     lax.fori_loop(0, R // BQ, q_block, 0)
 
 
-def attn_fwd(lo, hi, q, k, v, dq, dk, BQ=256, BK=256):
-    R, C = q.shape
+def attn_fwd(lo, hi, projected, tables, dq, dk, BQ=256, BK=256):
+    R = projected.shape[0]
+    C = projected.shape[1] // 3
     pairs = C // 128
     blk = pl.BlockSpec((R, 128), lambda p, *_: (0, p))
+    part = [pl.BlockSpec((R, 128), lambda p, *_, w=w: (0, w * pairs + p)) for w in range(3)]
+    fixed = pl.BlockSpec((R, 128), lambda p, *_: (0, 0))
+    half = jax.ShapeDtypeStruct((R, C), jnp.bfloat16)
     return pl.pallas_call(
         functools.partial(attn_fwd_body, BQ, BK),
-        out_shape=(jax.ShapeDtypeStruct((R, C), jnp.bfloat16), jax.ShapeDtypeStruct((R, C), jnp.float32)),
+        out_shape=(half, half, half, half, jax.ShapeDtypeStruct((R, C), jnp.float32)),
         grid_spec=pltpu.PrefetchScalarGridSpec(
             num_scalar_prefetch=2, grid=(pairs,),
-            in_specs=[blk, blk, blk, pl.BlockSpec((R, 1), lambda p, *_: (0, 0)), pl.BlockSpec((1, R), lambda p, *_: (0, 0))],
-            out_specs=[blk, blk]),
-        cost_estimate=pl.CostEstimate(flops=pairs * 2 * R * R * 64 * 4, bytes_accessed=R * C * 12, transcendentals=pairs * 2 * R * R),
+            in_specs=part + [fixed, fixed, pl.BlockSpec((R, 1), lambda p, *_: (0, 0)), pl.BlockSpec((1, R), lambda p, *_: (0, 0))],
+            out_specs=[blk] * 5),
+        cost_estimate=pl.CostEstimate(flops=pairs * 2 * R * R * 64 * 4, bytes_accessed=R * C * 24, transcendentals=pairs * 2 * R * R),
         name="attn_fwd",
-    )(lo, hi, q, k, v, dq, dk)
-
-
-def attn_bwd_body(BQ, BK, mode, lo_ref, hi_ref, q_ref, k_ref, v_ref, do_ref, o_ref, lse_ref, dq_ref, dk_ref,
-                  gq_ref, gk_ref, gv_ref, gq_s, lse_s, delta_s):
+    )(lo, hi, projected, projected, projected, *tables, dq, dk)
+
+
+def attn_bwd_body(BQ, BK, lo_ref, hi_ref, q_ref, k_ref, v_ref, do_ref, o_ref, lse_ref, cos_ref, sin_ref, dq_ref, dk_ref,
+                  gq_out, gk_out, gv_out, gk_ref, gv_ref):
     R = q_ref.shape[0]
     nq = R // BQ
     scale = HEAD_DIM ** (-0.5)
@@ -131,29 +152,39 @@
             gv_ref[cols, :] = gv
             return acc
 
-        gq_ref[rows, :] = lax.fori_loop(lo_ref[i], hi_ref[i], kv_block, jnp.zeros((BQ, 128), jnp.float32)) * scale
+        gq = lax.fori_loop(lo_ref[i], hi_ref[i], kv_block, jnp.zeros((BQ, 128), jnp.float32)) * scale
+        gq_out[rows, :] = turn(gq, cos_ref[rows, :], -sin_ref[rows, :]).astype(jnp.bfloat16)
         return 0
 
     lax.fori_loop(0, nq, q_block, 0)
-    gk_ref[...] = gk_ref[...] * scale
-
-
-def attn_bwd(lo, hi, q, k, v, do, o, lse, dqrow, dkcol, BQ=256, BK=256, mode=0):
+
+    def close_block(i, _):
+        rows = pl.ds(pl.multiple_of(i * 256, 256), 256)
+        gk = gk_ref[rows, :] * scale
+        gk_out[rows, :] = turn(gk, cos_ref[rows, :], -sin_ref[rows, :]).astype(jnp.bfloat16)
+        gv_out[rows, :] = gv_ref[rows, :].astype(jnp.bfloat16)
+        return 0
+
+    lax.fori_loop(0, R // 256, close_block, 0)
+
+
+def attn_bwd(lo, hi, q, k, v, do, o, lse, tables, dqrow, dkcol, BQ=256, BK=256):
     R, C = q.shape
     pairs = C // 128
     blk = pl.BlockSpec((R, 128), lambda p, *_: (0, p))
-    f32 = jax.ShapeDtypeStruct((R, C), jnp.float32)
+    fixed = pl.BlockSpec((R, 128), lambda p, *_: (0, 0))
+    half = jax.ShapeDtypeStruct((R, C), jnp.bfloat16)
     return pl.pallas_call(
-        functools.partial(attn_bwd_body, BQ, BK, mode),
-        out_shape=(f32, f32, f32),
+        functools.partial(attn_bwd_body, BQ, BK),
+        out_shape=(half, half, half),
         grid_spec=pltpu.PrefetchScalarGridSpec(
             num_scalar_prefetch=2, grid=(pairs,),
-            in_specs=[blk] * 6 + [pl.BlockSpec((1, R), lambda p, *_: (0, 0)), pl.BlockSpec((R, 1), lambda p, *_: (0, 0))],
+            in_specs=[blk] * 6 + [fixed, fixed, pl.BlockSpec((1, R), lambda p, *_: (0, 0)), pl.BlockSpec((R, 1), lambda p, *_: (0, 0))],
             out_specs=[blk, blk, blk],
-            scratch_shapes=[pltpu.VMEM((8, 128), jnp.float32)] * 3),
+            scratch_shapes=[pltpu.VMEM((R, 128), jnp.float32)] * 2),
         cost_estimate=pl.CostEstimate(flops=pairs * 2 * R * R * 64 * 10, bytes_accessed=R * C * 24, transcendentals=pairs * 2 * R * R),
         name="attn_bwd",
-    )(lo, hi, q, k, v, do, o, lse, dqrow, dkcol)
+    )(lo, hi, q, k, v, do, o, lse, *tables, dqrow, dkcol)
 
 
 def ranges(lens, R, BQ, BK):
@@ -185,14 +216,6 @@
     return jnp.cos(angles), jnp.sin(angles) * sign[None, :]
 
 
-def rotate(values, cosine, sine):
-    rows, width = values.shape
-    parts = values.reshape(rows, width // 64, 2, 32)
-    turned = jnp.stack([parts[:, :, 1], parts[:, :, 0]], axis=2).reshape(rows, width)
-    tiles = width // 128
-    return values * jnp.tile(cosine, (1, tiles)) + turned * jnp.tile(sine, (1, tiles))
-
-
 def layer_norm(summed, gain_row, bias_row):
     centred = summed - jnp.mean(summed, axis=-1, keepdims=True)
     inv_std = lax.rsqrt(jnp.mean(centred * centred, axis=-1, keepdims=True) + norm_eps)
@@ -220,12 +243,8 @@
 def forward_layer(x, xb, mats, norm_rows, tables, ids):
     wq, wo, wg, wd = mats
     lo, hi, col, row = ids
-    width = wo.shape[1]
     projected = dot(xb, wq, ((1,), (0,)))
-    q = rotate(projected[:, :width], *tables).astype(BF16)
-    k = rotate(projected[:, width : 2 * width], *tables).astype(BF16)
-    v = projected[:, 2 * width :].astype(BF16)
-    o, lse = attn_fwd(lo, hi, q, k, v, col, row, 512, 512)
+    q, k, v, o, lse = attn_fwd(lo, hi, projected, tables, col, row, 512, 512)
     a = both(dot(o, wo, ((1,), (1,))))
     h, n1, r1 = layer_norm(x + a, norm_rows[0], norm_rows[1])
     hb = h.astype(BF16)
@@ -261,9 +280,7 @@
     dzb1 = dz1.astype(BF16)
     g_proj = dot(dzb1, o, ((0,), (0,)))
     do = dot(dzb1, wo, ((1,), (0,))).astype(BF16)
-    gq, gk, gv = attn_bwd(lo, hi, q, k, v, do, o, lse, row, col, 512, 512)
-    cosine, sine = tables
-    dpb = jnp.concatenate([rotate(gq, cosine, -sine), rotate(gk, cosine, -sine), gv], axis=1).astype(BF16)
+    dpb = jnp.concatenate(attn_bwd(lo, hi, q, k, v, do, o, lse, tables, row, col, 512, 512), axis=1)
     g_qkv = dot(xb, dpb, ((0,), (0,)))
     dx = both(dot(dpb, wq, ((1,), (1,)))) + dz1
     return (g_qkv, g_proj, g_gate, g_down), jnp.stack([gain1, bias1, gain2, bias2]), dx
@@ -276,37 +293,37 @@
     return (gradient, weight_new, moment_new, average_new)
 
 
-def gather(shard):
-    own = lax.all_gather(shard, ("z", "y"), axis=0, tiled=True)
-    return own, swap(own, "tx")
-
-
-def pick(values, index, axis):
-    return lax.dynamic_index_in_dim(values, index, axis, keepdims=False)
-
-
-def halves(sheet, rows, y):
-    laid = sheet.reshape(-1, 2, rows, sheet.shape[-1])
-    return pick(laid, y, 1), pick(laid, 1 - y, 1)
-
-
-def scatter_x(own, other, rows):
-    y = lax.axis_index("y")
-    got = swap(other.astype(BF16), "tx")
-    keep, send = halves(own.astype(F32) + got.astype(F32), rows, y)
-    got = swap(send.astype(BF16), "y")
-    total = (keep + got.astype(F32)).astype(BF16)
-    return lax.psum_scatter(total.reshape(-1, total.shape[-1]), "z", scatter_dimension=0, tiled=True).astype(F32)
-
-
-def scatter_y(own, other, rows):
-    y = lax.axis_index("y")
-    keep_own, send_own = halves(own.astype(F32), rows, y)
-    keep_other, send_other = halves(other.astype(F32), rows, y)
-    got = swap(jnp.stack([send_own, send_other]).astype(BF16), "y").astype(F32)
-    far = swap((keep_other + got[1]).astype(BF16), "tx").astype(F32)
-    total = (keep_own + got[0] + far).astype(BF16)
-    return lax.psum_scatter(total.reshape(-1, total.shape[-1]), "z", scatter_dimension=0, tiled=True).astype(F32)
+def spread(values, widths):
+    far = swap(values, "tx")
+    cols, at = [], 0
+    for w in widths:
+        cols += [values[:, at : at + w], far[:, at : at + w]]
+        at += w
+    return lax.all_gather(jnp.concatenate(cols, axis=1), ("z", "y"), axis=0, tiled=True)
+
+
+def owners(partial, widths):
+    share = lax.psum_scatter(partial, ("z", "y"), scatter_dimension=0, tiled=True)
+    own, other, at = [], [], 0
+    for w in widths:
+        own.append(share[:, at : at + w])
+        other.append(share[:, at + w : at + 2 * w])
+        at += 2 * w
+    got = swap(jnp.concatenate(other, axis=1), "tx")
+    return jnp.concatenate(own, axis=1).astype(F32) + got.astype(F32)
+
+
+def total_over(values):
+    for axis in ("tx", "y"):
+        values = values + swap(values, axis)
+    count = lax.axis_size("z")
+    if count & (count - 1):
+        return lax.psum(values, "z")
+    step = 1
+    while step < count:
+        values = values + lax.ppermute(values, "z", [(i, i ^ step) for i in range(count)])
+        step *= 2
+    return values
 
 
 def per_device(
@@ -344,19 +361,11 @@
 
     mats = []
     for i in range(layers):
-        qkv, proj = qkv_weight[i], proj_weight[i]
-        sheets = gather(jnp.concatenate([qkv.reshape(rows, 3 * heads_w), proj], axis=1).astype(BF16))
-        gates = gather(gate_up_weight[i].reshape(rows, 2 * hid_w).astype(BF16))
-        downs = gather(down_weight[i].astype(BF16))
-
-        def side(w, first, count, each):
-            return jnp.concatenate(
-                [w[t][:, (first + c) * each : (first + c + 1) * each] for c in range(count) for t in range(2)], axis=1
-            )
-
-        mats.append((
-            side(sheets, 0, 3, heads_w), side(sheets, 3, 1, heads_w), side(gates, 0, 2, hid_w), side(downs, 0, 1, hid_w)
-        ))
+        heads = jnp.concatenate([qkv_weight[i].reshape(rows, 3 * heads_w), proj_weight[i]], axis=1).astype(BF16)
+        hidden = jnp.concatenate([gate_up_weight[i].reshape(rows, 2 * hid_w), down_weight[i]], axis=1).astype(BF16)
+        heads = spread(heads, [heads_w] * 4)
+        hidden = spread(hidden, [hid_w] * 3)
+        mats.append((heads[:, : 6 * heads_w], heads[:, 6 * heads_w :], hidden[:, : 4 * hid_w], hidden[:, 4 * hid_w :]))
 
     x = xb.astype(F32)
     stash = []
@@ -386,25 +395,17 @@
             grad, mats[i], norm_params[i], stash[i], tables, ids
         )
 
-        def sides(g, count, each):
-            return [
-                jnp.concatenate([g[:, (2 * c + t) * each : (2 * c + t + 1) * each] for c in range(count)], axis=1)
-                for t in range(2)
-            ]
-
-        gu, dn = sides(g_gate, 2, hid_w), sides(g_down, 1, hid_w)
-        qk, pr = sides(g_qkv, 3, heads_w), sides(g_proj, 1, heads_w)
-        share_d = scatter_y(dn[0], dn[1], rows)
-        share_g = scatter_x(gu[0], gu[1], rows)
-        share_a = scatter_y(*[jnp.concatenate([qk[t], pr[t]], axis=1) for t in range(2)], rows)
+        block = jnp.concatenate([g.astype(BF16) for g in (g_gate, g_down, g_proj)], axis=1)
+        block = owners(block, [hid_w] * 3 + [heads_w])
+        heads = owners(g_qkv.astype(BF16), [heads_w] * 3)
         shares[i] = (
-            share_a[:, : 3 * heads_w].reshape(rows, 3, heads_w),
-            share_a[:, 3 * heads_w :],
-            share_g.reshape(rows, 2, hid_w),
-            share_d,
+            heads.reshape(rows, 3, heads_w),
+            block[:, 3 * hid_w :],
+            block[:, : 2 * hid_w].reshape(rows, 2, hid_w),
+            block[:, 2 * hid_w : 3 * hid_w],
         )
     input_grad = arrivals(grad.astype(BF16))
-    norm_total = lax.psum(0.5 * jnp.stack(norm_sums), ("z", "y", "tx", "core"))
+    norm_total = total_over(jnp.stack(norm_sums))
 
     total_tokens = local_rows * 8 * lax.axis_size("z")
     proj_fan = max(1, D * 8 // SEQ_MOST)

time: 1140 us -> 1020 us (0.89)
  blocking collectives: 110 us -> 0 us
  local copies, waits for them, and re-layouts: 233 us -> 124 us
  waiting for transfers between devices: 242 us -> 339 us
  Pallas kernels: 122 us -> 213 us
  other arithmetic: 196 us -> 105 us
    reduce_scatter x6 -> x4, waiting for transfers between devices: 0.03 us -> 160 us  [owners(): lax.psum_scatter(partial, ('z', 'y'), scatter_dimension=0, tiled=True)]
    psum x1 -> x0, blocking collectives: 110 us -> none  [per_device(): norm_total = lax.psum(0.5 * jnp.stack(norm_sums), ('z', 'y', 'tx', 'core'))]
    ppermute x34 -> x26, waiting for transfers between devices: 236 us -> 134 us  [swap(): return lax.ppermute(values, axis, SWAP)]
    pallas_call x4, Pallas kernels: 122 us -> 213 us  [the longest x2 109 us: attn_bwd(): pl.pallas_call(functools.partial(attn_bwd_body, BQ, BK), out_shape=(half,...]
    slice x43 -> x12, local copies, waits for them, and re-layouts: 68.3 us -> 8.25 us  [the longest x6 7.42 us: owners(): own.append(share[:, at:at + w])]
    convert_element_type x18 -> x0, other arithmetic: 34.7 us -> none  [the longest x2 13.7 us: forward_layer(): k = rotate(projected[:, width:2 * width], *tables).astype(BF16)]
    all_gather x6 -> x4, waiting for transfers between devices: 5.03 us -> 38.9 us  [spread(): lax.all_gather(jnp.concatenate(cols, axis=1), ('z', 'y'), axis=0, tiled=T...]
    another operation x22 -> x7, other arithmetic: 33.4 us -> 1.88 us
  transfers between devices with their start and end apart: 46 -> 36, of which waited for: 16 -> 22; matrix products, arithmetic and copies ran while one was open for 47% -> 29% of each run, Pallas kernels for 11% -> 16%
where the time goes in v3:
time: 1020 us; the launch traced here: 1010 us
  waiting for transfers between devices  339 us (33%)
  Pallas kernels  213 us (21%)
  matrix products  197 us (19%)
  local copies, waits for them, and re-layouts  124 us (12%)
  other arithmetic  105 us (10%)
  starting transfers between devices  17.3 us (2%)
  between operations  17.1 us (2%)
    dot_general x24, matrix products, dot(): return lax.dot_general(a, b, (dims, ((), ())), preferred_element_type=F32)  197 us
    reduce_scatter x4, waiting for transfers between devices, owners(): lax.psum_scatter(partial, ('z', 'y'), scatter_dimension=0, tiled=True)  160 us
    ppermute x26, waiting for transfers between devices, swap(): return lax.ppermute(values, axis, SWAP)  134 us
    pallas_call x2, Pallas kernels, attn_bwd(): pl.pallas_call(functools.partial(attn_bwd_body, BQ, BK), out_shape=(half,...  109 us
    pallas_call x2, Pallas kernels, attn_fwd(): pl.pallas_call(functools.partial(attn_fwd_body, BQ, BK), out_shape=(half,...  103 us
    unnamed x207, local copies, waits for them, and re-layouts  51.3 us
    all_gather x4, waiting for transfers between devices, spread(): lax.all_gather(jnp.concatenate(cols, axis=1), ('z', 'y'), axis=0, tiled=T...  38.9 us
  transfers between devices with their start and end apart: 36, of which 22 were waited for; matrix products, arithmetic and copies ran while one was open for 29% of the time, Pallas kernels for 16%

profile of v3, /device:TPU:0, one launch (start us, length us, event | category | flops | bytes accessed | tf_op | source)
XLA Modules:
  0.0 1012.4 jit_solution(8332012827001322810)
XLA Ops:
  27.1 10.8 %collective-permute-done.8 = bf16[96,2304]{1,0:T(8,128)(2,1)S(1)} collective-permute-done((bf16[96,2304]{1,0:T(8,128)(2,1)S(1)}, bf16[96,2304]{1,0:T(8,128)(2,1)S(1)}, u32[]{:S(2)}, u32[]{:S(2)}) %collective-permute-start.8) | collective-permute-done | bytes 442400 | tf_op jit(solution)/shard_map/ppermute | solution.py:208
  48.5 24.9 %collective-permute-done = bf16[768,768]{1,0:T(8,128)(2,1)S(1)} collective-permute-done((bf16[768,768]{1,0:T(8,128)(2,1)S(1)}, bf16[768,768]{1,0:T(8,128)(2,1)S(1)}, u32[]{:S(2)}, u32[]{:S(2)}) %collective-permute-start) | collective-permute-done | bytes 1179680 | tf_op jit(solution)/shard_map/ppermute | solution.py:208
  106.6 51.7 %attn_fwd.2 = (bf16[1536,384]{1,0:T(8,128)(2,1)}, bf16[1536,384]{1,0:T(8,128)(2,1)}, bf16[1536,384]{1,0:T(8,128)(2,1)}, bf16[1536,384]{1,0:T(8,128)(2,1)}, f32[1536,384]{1,0:T(8,128)}) custom-call(s32[3]{0:T(128)} %get-tuple-element.228.lo_ref, s32[3]{0:T(128)} %get-tuple-element.227.hi_ref, f32[1536,1152]{1,0:T(8,128)} %fusion.38.pq_ref.pk_ref.pv_ref, ...), custom_call_target="tpu_custom_call" | custom-call | flops 3623878656 | bytes 14155776 | tf_op jit(solution)/shard_map/attn_fwd/pallas_call | solution.py:98
  174.3 11.9 %all-gather.7.cloned.1.call-done = bf16[768,4608]{1,0:T(8,128)(2,1)} async-done(((bf16[96,4608]{1,0:T(8,128)(2,1)}), bf16[768,4608]{1,0:T(8,128)(2,1)}) %all-gather.7.cloned.1.call-update) | async-done | bytes 7077904 | tf_op jit(solution)/shard_map/all_gather | solution.py:302
  186.3 11.5 %fusion.20 = f32[1536,3072]{1,0:T(8,128)S(1)} fusion(bf16[768,4608]{1,0:T(8,128)(2,1)} %all-gather.7.cloned.1.call-done, f32[1536,768]{0,1:T(8,128)} %copy-done.2, f32[768]{0:T(1024)S(1)} %get-tuple-element.141, f32[768]{0:T(1024)S(1)} %get-tuple-element.142, f32[1536]{0:T(1024)S(1)} %add_rsqrt_fusion.3, f32[1536]{0:T(1024)S(1)} %broadcast_multiply_fusion.11), kind=kOutput, calls=%fused_computation.72 | convolution fusion | flops 7253655552 | bytes 28329984 | tf_op jit(solution)/shard_map/dot_general | solution.py:234
  222.4 16.6 %all-gather.9.cloned.1.call-done = bf16[768,1536]{1,0:T(8,128)(2,1)} async-done(((bf16[96,1536]{1,0:T(8,128)(2,1)}), bf16[768,1536]{1,0:T(8,128)(2,1)}) %all-gather.9.cloned.1.call-update) | async-done | bytes 2359312 | tf_op jit(solution)/shard_map/all_gather | solution.py:302
  239.1 9.4 fusion.35.pq_ref.pk_ref.pv_ref
  248.5 51.7 %attn_fwd.3 = (bf16[1536,384]{1,0:T(8,128)(2,1)}, bf16[1536,384]{1,0:T(8,128)(2,1)}, bf16[1536,384]{1,0:T(8,128)(2,1)}, bf16[1536,384]{1,0:T(8,128)(2,1)}, f32[1536,384]{1,0:T(8,128)}) custom-call(s32[3]{0:T(128)} %get-tuple-element.228.lo_ref, s32[3]{0:T(128)} %get-tuple-element.227.hi_ref, f32[1536,1152]{1,0:T(8,128)} %fusion.35.pq_ref.pk_ref.pv_ref, ...), custom_call_target="tpu_custom_call" | custom-call | flops 3623878656 | bytes 14155776 | tf_op jit(solution)/shard_map/attn_fwd/pallas_call | solution.py:98
  303.4 28.3 %collective-permute-done.12 = bf16[768,768]{1,0:T(8,128)(2,1)S(1)} collective-permute-done((bf16[768,768]{1,0:T(8,128)(2,1)S(1)}, bf16[768,768]{1,0:T(8,128)(2,1)S(1)}, u32[]{:S(2)}, u32[]{:S(2)}) %collective-permute-start.12) | collective-permute-done | bytes 1179680 | tf_op jit(solution)/shard_map/ppermute | solution.py:208
  337.7 10.3 %all-gather.11.cloned.1.call-done = bf16[768,4608]{1,0:T(8,128)(2,1)} async-done(((bf16[96,4608]{1,0:T(8,128)(2,1)}), bf16[768,4608]{1,0:T(8,128)(2,1)}) %all-gather.11.cloned.1.call-update) | async-done | bytes 7077904 | tf_op jit(solution)/shard_map/all_gather | solution.py:302
  348.0 11.9 %fusion.17 = f32[1536,3072]{1,0:T(8,128)S(1)} fusion(bf16[768,4608]{1,0:T(8,128)(2,1)} %all-gather.11.cloned.1.call-done, f32[1536,768]{0,1:T(8,128)} %copy-done.3, f32[768]{0:T(1024)S(1)} %get-tuple-element.137, f32[768]{0:T(1024)S(1)} %get-tuple-element.138, f32[1536]{0:T(1024)S(1)} %add_rsqrt_fusion.1, f32[1536]{0:T(1024)S(1)} %broadcast_multiply_fusion.9), kind=kOutput, calls=%fused_computation.69 | convolution fusion | flops 7253655552 | bytes 28329984 | tf_op jit(solution)/shard_map/dot_general | solution.py:234
  401.1 16.5 %multiply_convert_fusion.3 = (bf16[1536,1536]{1,0:T(8,128)(2,1)}, bf16[1536,1536]{1,0:T(8,128)(2,1)}) fusion(f32[1536,3072]{1,0:T(8,128)} %copy-done.12, bf16[768,4608]{1,0:T(8,128)(2,1)} %all-gather.11.cloned.1.call-done, f32[1536]{0:T(1024)S(1)} %broadcast_multiply_fusion.6, f32[1536,768]{0,1:T(8,128)S(1)} %get-tuple-element.167, ...), kind=kOutput, calls=%fused_computation.9 | convolution fusion | flops 3665166336 | bytes 37776384 | tf_op jit(solution)/shard_map/dot_general | solution.py:234
  417.6 11.7 %fusion.22 = bf16[1536,768]{0,1:T(8,128)(2,1)S(1)} fusion(bf16[768,4608]{1,0:T(8,128)(2,1)} %all-gather.11.cloned.1.call-done, bf16[1536,1536]{1,0:T(8,128)(2,1)} %get-tuple-element.177, bf16[1536,1536]{1,0:T(8,128)(2,1)} %get-tuple-element.176), kind=kOutput, calls=%fused_computation.77 | convolution fusion | flops 7267811328 | bytes 16515072 | tf_op jit(solution)/shard_map/dot_general | solution.py:234
  446.8 54.5 %attn_bwd.2 = (bf16[1536,384]{1,0:T(8,128)(2,1)}, bf16[1536,384]{1,0:T(8,128)(2,1)}, bf16[1536,384]{1,0:T(8,128)(2,1)}) custom-call(s32[3]{0:T(128)} %get-tuple-element.228.lo_ref, s32[3]{0:T(128)} %get-tuple-element.227.hi_ref, bf16[1536,384]{1,0:T(8,128)(2,1)} %get-tuple-element.43.q_ref, bf16[1536,384]{1,0:T(8,128)(2,1)} %get-tuple-element.44.k_ref, ...), custom_call_target="tpu_custom_call" | custom-call | flops 9059696640 | bytes 14155776 | tf_op jit(solution)/shard_map/attn_bwd/pallas_call | solution.py:177
  519.7 17.0 %multiply_convert_fusion.1 = (bf16[1536,1536]{1,0:T(8,128)(2,1)}, bf16[1536,1536]{1,0:T(8,128)(2,1)}) fusion(f32[1536,3072]{1,0:T(8,128)} %copy-done.11, bf16[768,4608]{1,0:T(8,128)(2,1)} %all-gather.7.cloned.1.call-done, f32[1536,768]{0,1:T(8,128)S(1)} %subtract_multiply_fusion.1), kind=kOutput, calls=%fused_computation.7 | convolution fusion | flops 3655729152 | bytes 35389440 | tf_op jit(solution)/shard_map/dot_general | solution.py:234
  536.8 11.7 %fusion.25 = bf16[1536,768]{0,1:T(8,128)(2,1)S(1)} fusion(bf16[768,4608]{1,0:T(8,128)(2,1)} %all-gather.7.cloned.1.call-done, bf16[1536,1536]{1,0:T(8,128)(2,1)} %get-tuple-element.175, bf16[1536,1536]{1,0:T(8,128)(2,1)} %get-tuple-element.174), kind=kOutput, calls=%fused_computation.78 | convolution fusion | flops 7267811328 | bytes 16515072 | tf_op jit(solution)/shard_map/dot_general | solution.py:234
  570.0 54.5 %attn_bwd.3 = (bf16[1536,384]{1,0:T(8,128)(2,1)}, bf16[1536,384]{1,0:T(8,128)(2,1)}, bf16[1536,384]{1,0:T(8,128)(2,1)}) custom-call(s32[3]{0:T(128)} %get-tuple-element.228.lo_ref, s32[3]{0:T(128)} %get-tuple-element.227.hi_ref, bf16[1536,384]{1,0:T(8,128)(2,1)} %get-tuple-element.40.q_ref, bf16[1536,384]{1,0:T(8,128)(2,1)} %get-tuple-element.41.k_ref, ...), custom_call_target="tpu_custom_call" | custom-call | flops 9059696640 | bytes 14155776 | tf_op jit(solution)/shard_map/attn_bwd/pallas_call | solution.py:177
  634.5 9.4 convolution_convert_fusion
  643.8 12.9 %fusion.7 = bf16[768,3072]{1,0:T(8,128)(2,1)S(1)} fusion(bf16[1536,1536]{1,0:T(8,128)(2,1)} %get-tuple-element.177, bf16[1536,1536]{1,0:T(8,128)(2,1)} %get-tuple-element.176, f32[1536,768]{0,1:T(8,128)} %copy-done.3, f32[768]{0:T(1024)S(1)} %copy-done.59, f32[768]{0:T(1024)S(1)} %get-tuple-element.138, f32[1536]{0:T(1024)S(1)} %add_rsqrt_fusion.1, ...), kind=kOutput, calls=%fused_computation.26 | convolution fusion | flops 7274889216 | bytes 18892800 | tf_op jit(solution)/shard_map/dot_general | solution.py:234
  663.4 9.2 convolution_convert_fusion.1
  672.6 12.8 %fusion.8 = bf16[768,3072]{1,0:T(8,128)(2,1)S(1)} fusion(bf16[1536,1536]{1,0:T(8,128)(2,1)} %get-tuple-element.175, bf16[1536,1536]{1,0:T(8,128)(2,1)} %get-tuple-element.174, f32[1536,768]{0,1:T(8,128)} %copy-done.2, f32[768]{0:T(1024)S(1)} %copy-done.57, f32[768]{0:T(1024)S(1)} %copy-done.55, f32[1536]{0:T(1024)S(1)} %copy-done.52, f32[1536]{0:T(1024)S(1)} %copy-done.47), kind=kOutput, calls=%fused_computation.27 | convolution fusion | flops 7274889216 | bytes 18892800 | tf_op jit(solution)/shard_map/dot_general | solution.py:234
  701.2 20.7 %collective-permute-done.10 = bf16[768,768]{0,1:T(8,128)(2,1)} collective-permute-done((bf16[768,768]{0,1:T(8,128)(2,1)S(1)}, bf16[768,768]{0,1:T(8,128)(2,1)}, u32[]{:S(2)}, u32[]{:S(2)}) %collective-permute-start.10) | collective-permute-done | bytes 1179680 | tf_op jit(solution)/shard_map/ppermute | solution.py:208
  815.7 22.7 %reduce-scatter.11.cloned.1.call-done = bf16[96,4992]{1,0:T(8,128)(2,1)} async-done(((bf16[768,4992]{1,0:T(8,128)(2,1)}), bf16[96,4992]{1,0:T(8,128)(2,1)}) %reduce-scatter.11.cloned.1.call-update) | async-done | bytes 958480 | tf_op jit(solution)/shard_map/reduce_scatter | solution.py:306
  842.3 136.9 %reduce-scatter.9.cloned.1.call-done = bf16[96,4992]{1,0:T(8,128)(2,1)} async-done(((bf16[768,4992]{1,0:T(8,128)(2,1)}), bf16[96,4992]{1,0:T(8,128)(2,1)}) %reduce-scatter.9.cloned.1.call-update) | async-done | bytes 958480 | tf_op jit(solution)/shard_map/reduce_scatter | solution.py:306
  (437 shorter events, 365.7 us)
Async XLA Ops:
  7.2 91.9 %all-gather.5.cloned.1.call-start = ((), (), s32[]{:S(2)}) async-start(), calls=%async_computation.4 | async-start | bytes 2654208 | tf_op jit(solution)/shard_map/all_gather | solution.py:302
  13.0 8.9 collective-permute-start.2
  23.8 162.5 %all-gather.7.cloned.1.call-start = ((), (), s32[]{:S(2)}) async-start(), calls=%async_computation.5 | async-start | bytes 7962624 | tf_op jit(solution)/shard_map/all_gather | solution.py:302
  24.8 13.1 %collective-permute-start.8 = (bf16[96,2304]{1,0:T(8,128)(2,1)S(1)}, bf16[96,2304]{1,0:T(8,128)(2,1)S(1)}, u32[]{:S(2)}, u32[]{:S(2)}) collective-permute-start(bf16[96,2304]{1,0:T(8,128)(2,1)S(1)} %pad_maximum_fusion.27), channel_id=1, source_target_pairs={{0,2},{2,0},{1,3},{3,1},{4,6},{6,4},{5,7},{7,5},{8,10},{10,8},{9,1... | collective-permute-start | bytes 1327112 | tf_op jit(solution)/shard_map/ppermute | solution.py:208
  26.7 19.0 %collective-permute-start.4 = (bf16[96,2304]{1,0:T(8,128)(2,1)S(1)}, bf16[96,2304]{1,0:T(8,128)(2,1)S(1)}, u32[]{:S(2)}, u32[]{:S(2)}) collective-permute-start(bf16[96,2304]{1,0:T(8,128)(2,1)S(1)} %pad_maximum_fusion.26), channel_id=1, source_target_pairs={{0,2},{2,0},{1,3},{3,1},{4,6},{6,4},{5,7},{7,5},{8,10},{10,8},{9,1... | collective-permute-start | bytes 1327112 | tf_op jit(solution)/shard_map/ppermute | solution.py:208
  47.1 192.0 %all-gather.9.cloned.1.call-start = ((), (), s32[]{:S(2)}) async-start(), calls=%async_computation.6 | async-start | bytes 2654208 | tf_op jit(solution)/shard_map/all_gather | solution.py:302
  47.1 26.4 %collective-permute-start = (bf16[768,768]{1,0:T(8,128)(2,1)S(1)}, bf16[768,768]{1,0:T(8,128)(2,1)S(1)}, u32[]{:S(2)}, u32[]{:S(2)}) collective-permute-start(bf16[768,768]{1,0:T(8,128)(2,1)S(1)} %copy-done.19), channel_id=1, source_target_pairs={{0,2},{2,0},{1,3},{3,1},{4,6},{6,4},{5,7},{7,5},{8,10},{10,8},{9,1... | collective-permute-start | bytes 3538952 | tf_op jit(solution)/shard_map/ppermute | solution.py:208
  75.0 11.2 %collective-permute-start.1 = (bf16[1536,768]{1,0:T(8,128)(2,1)}, bf16[1536,768]{1,0:T(8,128)(2,1)}, u32[]{:S(2)}, u32[]{:S(2)}) collective-permute-start(bf16[1536,768]{1,0:T(8,128)(2,1)} %pad_maximum_fusion.20), channel_id=1, source_target_pairs={{0,1},{1,0},{2,3},{3,2},{4,5},{5,4},{6,7},{7,6},{8,9},{9,8},{10,11... | collective-permute-start | bytes 7077896 | tf_op jit(solution)/shard_map/ppermute | solution.py:208
  84.4 263.6 %all-gather.11.cloned.1.call-start = ((), (), s32[]{:S(2)}) async-start(), calls=%async_computation.7 | async-start | bytes 7962624 | tf_op jit(solution)/shard_map/all_gather | solution.py:302
  164.8 595.5 %reduce-scatter.7.cloned.1.call-start = ((), (), s32[]{:S(2)}) async-start(), calls=%async_computation.9 | async-start | bytes 1990656 | tf_op jit(solution)/shard_map/reduce_scatter | solution.py:306
  303.2 30.0 %collective-permute-start.7 = (bf16[1536,768]{0,1:T(8,128)(2,1)S(1)}, bf16[1536,768]{0,1:T(8,128)(2,1)S(1)}, u32[]{:S(2)}, u32[]{:S(2)}) collective-permute-start(bf16[1536,768]{0,1:T(8,128)(2,1)S(1)} %convolution_convert_fusion.8), channel_id=1, source_target_pairs={{0,1},{1,0},{2,3},{3,2},{4,5},{5,4},{6,7},{7,6},{8,9},{9,8},{10,11... | collective-permute-start | bytes 7077896 | tf_op jit(solution)/shard_map/ppermute | solution.py:208
  303.3 28.4 %collective-permute-start.12 = (bf16[768,768]{1,0:T(8,128)(2,1)S(1)}, bf16[768,768]{1,0:T(8,128)(2,1)S(1)}, u32[]{:S(2)}, u32[]{:S(2)}) collective-permute-start(bf16[768,768]{1,0:T(8,128)(2,1)S(1)} %copy-done.20), channel_id=1, source_target_pairs={{0,2},{2,0},{1,3},{3,1},{4,6},{6,4},{5,7},{7,5},{8,10},{10,8},{9,1... | collective-permute-start | bytes 3538952 | tf_op jit(solution)/shard_map/ppermute | solution.py:208
  333.3 41.6 %collective-permute-start.13 = (bf16[1536,768]{1,0:T(8,128)(2,1)}, bf16[1536,768]{1,0:T(8,128)(2,1)}, u32[]{:S(2)}, u32[]{:S(2)}) collective-permute-start(bf16[1536,768]{1,0:T(8,128)(2,1)} %pad_maximum_fusion.21), channel_id=1, source_target_pairs={{0,1},{1,0},{2,3},{3,2},{4,5},{5,4},{6,7},{7,6},{8,9},{9,8},{10,11... | collective-permute-start | bytes 7077896 | tf_op jit(solution)/shard_map/ppermute | solution.py:208
  374.9 15.2 %collective-permute-start.9 = (bf16[1536,768]{0,1:T(8,128)(2,1)}, bf16[1536,768]{0,1:T(8,128)(2,1)}, u32[]{:S(2)}, u32[]{:S(2)}) collective-permute-start(bf16[1536,768]{0,1:T(8,128)(2,1)} %convolution_convert_fusion.6), channel_id=1, source_target_pairs={{0,1},{1,0},{2,3},{3,2},{4,5},{5,4},{6,7},{7,6},{8,9},{9,8},{10,11... | collective-permute-start | bytes 7077896 | tf_op jit(solution)/shard_map/ppermute | solution.py:208
  554.1 224.3 %reduce-scatter.5.cloned.1.call-start = ((), (), s32[]{:S(2)}) async-start(), calls=%async_computation.8 | async-start | bytes 1990656 | tf_op jit(solution)/shard_map/reduce_scatter | solution.py:306
  634.2 204.2 %reduce-scatter.11.cloned.1.call-start = ((), (), s32[]{:S(2)}) async-start(), calls=%async_computation.11 | async-start | bytes 8626176 | tf_op jit(solution)/shard_map/reduce_scatter | solution.py:306
  663.1 316.0 %reduce-scatter.9.cloned.1.call-start = ((), (), s32[]{:S(2)}) async-start(), calls=%async_computation.10 | async-start | bytes 8626176 | tf_op jit(solution)/shard_map/reduce_scatter | solution.py:306
  693.7 28.1 %collective-permute-start.10 = (bf16[768,768]{0,1:T(8,128)(2,1)S(1)}, bf16[768,768]{0,1:T(8,128)(2,1)}, u32[]{:S(2)}, u32[]{:S(2)}) collective-permute-start(bf16[768,768]{0,1:T(8,128)(2,1)S(1)} %constant_dynamic-slice_fusion), channel_id=1, source_target_pairs={{0,2},{2,0},{1,3},{3,1},{4,6},{6,4},{5,7},{7,5},{8,10},{10,8},{9,1... | collective-permute-start | bytes 3538952 | tf_op jit(solution)/shard_map/ppermute | solution.py:208
  701.1 32.1 %collective-permute-start.17 = (bf16[1536,768]{0,1:T(8,128)(2,1)}, bf16[1536,768]{0,1:T(8,128)(2,1)}, u32[]{:S(2)}, u32[]{:S(2)}) collective-permute-start(bf16[1536,768]{0,1:T(8,128)(2,1)} %convolution_convert_fusion.4), channel_id=1, source_target_pairs={{0,1},{1,0},{2,3},{3,2},{4,5},{5,4},{6,7},{7,6},{8,9},{9,8},{10,11... | collective-permute-start | bytes 7077896 | tf_op jit(solution)/shard_map/ppermute | solution.py:208
  740.6 33.9 %collective-permute-start.18 = (bf16[768,768]{0,1:T(8,128)(2,1)}, bf16[768,768]{0,1:T(8,128)(2,1)}, u32[]{:S(2)}, u32[]{:S(2)}) collective-permute-start(bf16[768,768]{0,1:T(8,128)(2,1)} %constant_dynamic-slice_fusion.1), channel_id=1, source_target_pairs={{0,2},{2,0},{1,3},{3,1},{4,6},{6,4},{5,7},{7,5},{8,10},{10,8},{9,1... | collective-permute-start | bytes 3538952 | tf_op jit(solution)/shard_map/ppermute | solution.py:208
  758.2 11.6 %collective-permute-start.24 = (f32[2,4,768]{2,1,0:T(4,128)S(1)}, f32[2,4,768]{2,1,0:T(4,128)S(1)}, u32[]{:S(2)}, u32[]{:S(2)}) collective-permute-start(f32[2,4,768]{2,1,0:T(4,128)S(1)} %pad_maximum_fusion.33), channel_id=1, source_target_pairs={{0,2},{2,0},{1,3},{3,1},{4,6},{6,4},{5,7},{7,5},{8,10},{10,8},{9,1... | collective-permute-start | bytes 73736 | tf_op jit(solution)/shard_map/ppermute | solution.py:208
  774.5 20.6 %collective-permute-start.19 = (bf16[768,768]{0,1:T(8,128)(2,1)}, bf16[768,768]{0,1:T(8,128)(2,1)}, u32[]{:S(2)}, u32[]{:S(2)}) collective-permute-start(bf16[768,768]{0,1:T(8,128)(2,1)} %collective-permute-done.18), channel_id=1, source_target_pairs={{0,1},{1,0},{2,3},{3,2},{4,5},{5,4},{6,7},{7,6},{8,9},{9,8},{10,11... | collective-permute-start | bytes 3538952 | tf_op jit(solution)/shard_map/ppermute | solution.py:208
  840.7 143.7 %collective-permute-start.23 = (bf16[96,2496]{1,0:T(8,128)(2,1)S(1)}, bf16[96,2496]{1,0:T(8,128)(2,1)S(1)}, u32[]{:S(2)}, u32[]{:S(2)}) collective-permute-start(bf16[96,2496]{1,0:T(8,128)(2,1)S(1)} %pad_maximum_fusion.25), channel_id=1, source_target_pairs={{0,2},{2,0},{1,3},{3,1},{4,6},{6,4},{5,7},{7,5},{8,10},{10,8},{9,1... | collective-permute-start | bytes 1437704 | tf_op jit(solution)/shard_map/ppermute | solution.py:208
  982.9 12.3 %collective-permute-start.22 = (bf16[96,2496]{1,0:T(8,128)(2,1)}, bf16[96,2496]{1,0:T(8,128)(2,1)}, u32[]{:S(2)}, u32[]{:S(2)}) collective-permute-start(bf16[96,2496]{1,0:T(8,128)(2,1)} %pad_maximum_fusion.24), channel_id=1, source_target_pairs={{0,2},{2,0},{1,3},{3,1},{4,6},{6,4},{5,7},{7,5},{8,10},{10,8},{9,1... | collective-permute-start | bytes 1437704 | tf_op jit(solution)/shard_map/ppermute | solution.py:208
  (97 other events, 1734.1 us)
Sparse Core Ops, SparseCore 0:
  23.9 53.3 all-gather.4
  79.4 106.7 all-gather.6
  189.0 50.0 all-gather.8
  241.1 106.8 all-gather.10
  554.2 63.7 reduce-scatter.6
  634.3 63.8 reduce-scatter.4
  701.8 136.5 reduce-scatter.10
  842.0 137.0 reduce-scatter.8
